TPU v7x, 256 devices: a whole 4x4x8 slice. The times are simulated.
256 devices in a mesh: oct: 16 (over y, x), cube: 16 (over z, core).
Axes of the slice: x: 4, y: 4, z: 8, core: 2. Of those that a mesh axis runs over, the one named last changes fastest.
Arguments:
- charges: bfloat16 [65536, 128], P(('oct', 'cube')), may hold values from -6 to 6
- panel_counts: int32 [65536], P(('oct', 'cube')), may hold values from 32 to 128
- positions: float32 [3, 65536, 128], P(None, ('oct', 'cube')), may hold values from 0 to 2
- moment_map: bfloat16 [128, 128], replicated, may hold values from -0.5 to 0.5
- translations: bfloat16 [16, 128, 128], replicated, may hold values from -0.15625 to 0.15625
- evaluation: bfloat16 [128, 128], replicated, may hold values from -0.5 to 0.5
- near_boxes: int32 [65536, 4], P(('oct', 'cube')), may hold values from 0 to 255
- group_sources: int32 [65536, 8], P(('oct', 'cube')), may hold values from 0 to 4095
- group_patterns: int32 [65536, 8], P(('oct', 'cube')), may hold values from 0 to 15
- remote_sources: int32 [16, 16, 16, 64, 4], P('oct', 'cube'), may hold values from 0 to 255
- remote_patterns: int32 [16, 16, 16, 64, 4], P('oct', 'cube'), may hold values from 0 to 15
- remote_targets: int32 [16, 16, 16, 64], P('oct', 'cube'), may hold values from 0 to 255
Outputs:
- potential: float32 [65536, 128], P(('oct', 'cube'))
All inputs are finite; a program needn't handle non-finite values.
Results may differ from a plain program's by a relative error of at most 0.0024.
Values may be sent and summed in bfloat16 or wider, within the bound.
A program may use at most 64 MiB of HBM per device.

v0:
```python
import math

import jax
import jax.numpy as jnp
from jax import lax
from jax.sharding import PartitionSpec as P


def pattern_sums(rows, patterns, count):
    onehot = (patterns[..., None] == jnp.arange(count, dtype=jnp.int32)).astype(jnp.bfloat16)
    summed = jnp.einsum("nkp,nkc->npc", onehot, rows, preferred_element_type=jnp.float32)
    return summed.astype(jnp.bfloat16).reshape(rows.shape[0], count * rows.shape[2])


def near_block(args):
    target_pos, source_pos, source_q = args
    diffs = target_pos[:, :, None, :, None] - source_pos[:, :, :, None, :]
    dist_sq = jnp.sum(diffs * diffs, axis=0) + 0.0025
    kernel = source_q[:, :, None, :] * lax.rsqrt(dist_sq)
    return jnp.sum(kernel, axis=(1, 3))


def body(
    charges,
    panel_counts,
    positions,
    moment_map,
    translations,
    evaluation,
    near_boxes,
    group_sources,
    group_patterns,
    remote_sources,
    remote_patterns,
    remote_targets,
):
    boxes = charges.shape[0]
    panels = charges.shape[1]
    width = moment_map.shape[1]
    operator_count = translations.shape[0]
    operators = translations.reshape(operator_count * width, width)
    slot_index = jnp.arange(panels, dtype=jnp.int32)
    live = slot_index[None, :] < panel_counts[:, None]
    strength = jnp.where(live, charges, jnp.zeros_like(charges))
    multipole = jnp.dot(strength, moment_map, preferred_element_type=jnp.float32).astype(
        jnp.bfloat16
    )
    group_all = lax.all_gather(multipole, "cube", axis=0, tiled=True)
    group_sum = pattern_sums(group_all[group_sources], group_patterns, operator_count)
    near_local = jnp.dot(group_sum, operators, preferred_element_type=jnp.float32)
    sources = remote_sources[0, 0]
    patterns = remote_patterns[0, 0]
    targets = remote_targets[0, 0]
    groups = sources.shape[0]
    slots = sources.shape[1]
    fanin = sources.shape[2]
    rows = multipole[sources.reshape(-1)].reshape(groups, slots, fanin, width)
    got_rows = lax.all_to_all(rows, "oct", split_axis=0, concat_axis=0, tiled=True)
    got_patterns = lax.all_to_all(patterns, "oct", split_axis=0, concat_axis=0, tiled=True)
    got_targets = lax.all_to_all(targets, "oct", split_axis=0, concat_axis=0, tiled=True)
    count = got_rows.shape[1]
    flat = pattern_sums(
        got_rows.reshape(-1, fanin, width), got_patterns.reshape(-1, fanin), operator_count
    )
    result = jnp.dot(flat, operators, preferred_element_type=jnp.float32)
    received, got_targets = (result.reshape(groups, count, width), got_targets)
    remote_local = jax.ops.segment_sum(
        received.reshape(-1, width), got_targets.reshape(-1), num_segments=boxes
    )
    local = (near_local + remote_local).astype(jnp.bfloat16)
    far = jnp.dot(local, evaluation, preferred_element_type=jnp.float32)
    block = min(boxes, 16)
    count = boxes // block
    strength_f = strength.astype(jnp.float32)
    target_pos = positions.reshape(3, count, block, panels).transpose(1, 0, 2, 3)
    flat_near = near_boxes.reshape(-1)
    knear = near_boxes.shape[1]
    source_pos = (
        positions[:, flat_near].reshape(3, count, block, knear, panels).transpose(1, 0, 2, 3, 4)
    )
    source_q = strength_f[flat_near].reshape(count, block, knear, panels)
    near = lax.map(near_block, (target_pos, source_pos, source_q)).reshape(boxes, panels)
    total = near * (1.0 / (4.0 * math.pi)) + far
    return jnp.where(live, total, jnp.zeros_like(total))


def solution(mesh):
    return jax.shard_map(
        body,
        mesh=mesh,
        in_specs=(
            P(("oct", "cube"), None),
            P(("oct", "cube")),
            P(None, ("oct", "cube"), None),
            P(),
            P(),
            P(),
            P(("oct", "cube"), None),
            P(("oct", "cube"), None),
            P(("oct", "cube"), None),
            P("oct", "cube", None, None, None),
            P("oct", "cube", None, None, None),
            P("oct", "cube", None, None),
        ),
        out_specs=P(("oct", "cube"), None),
        check_vma=False,
    )
```

profile of v0, /device:TPU:1, one launch (start us, length us, event | category | flops | bytes accessed | tf_op | source)
XLA Modules:
  0.0 157.0 jit_solution(9919311703684641480)
XLA Ops:
  6.5 1.8 %convolution_convert_fusion.2 = bf16[256,128]{1,0:T(8,128)(2,1)} fusion(bf16[128,128]{1,0:T(8,128)(2,1)} %param.17, bf16[256,128]{1,0:T(8,128)(2,1)} %param.14, s32[256]{0:T(256)} %param.15), kind=kOutput, calls=%fused_computation.20 | convolution fusion | flops 8486912 | bytes 164864 | tf_op jit(solution)/shard_map/dot_general | solution.py:45
  8.4 7.6 %all-to-all-start = ((s32[16,1,64]{2,1,0:T(1,128)}), s32[16,1,64]{2,1,0:T(1,128)S(1)}, u32[]{:S(2)}, u32[]{:S(2)}) async-start(s32[16,1,64]{2,1,0:T(1,128)} %bitcast.63), calls=%async_computation | async-start | bytes 16384 | tf_op jit(solution)/shard_map/all_to_all | solution.py:60
  16.0 0.9 fusion.13
  17.9 1.0 copy.40
  20.7 1.6 %all-to-all-done = s32[16,1,64]{2,1,0:T(1,128)S(1)} async-done(((s32[16,1,64]{2,1,0:T(1,128)}), s32[16,1,64]{2,1,0:T(1,128)S(1)}, u32[]{:S(2)}, u32[]{:S(2)}) %all-to-all-start) | async-done | bytes 4128 | tf_op jit(solution)/shard_map/all_to_all | solution.py:60
  22.3 5.1 %all-to-all-start.1 = ((s32[16,1,256]{2,1,0:T(1,128)}), s32[16,1,256]{2,1,0:T(1,128)S(1)}, u32[]{:S(2)}, u32[]{:S(2)}) async-start(s32[16,1,256]{2,1,0:T(1,128)} %reshape.153), calls=%async_computation.1 | async-start | bytes 32768 | tf_op jit(solution)/shard_map/all_to_all | solution.py:59
  27.4 2.8 %gather_fusion = f32[1024,128]{1,0:T(8,128)S(1)} fusion(f32[256,128]{1,0:T(8,128)S(1)} %fusion.13, s32[1024]{0:T(1024)S(1)} %broadcast_clamp_fusion.2), kind=kCustom, calls=%fused_computation | custom fusion | bytes 1052672 | tf_op jit(solution)/shard_map/gather | solution.py:81
  30.3 3.9 %gather_fusion.1 = f32[1024,3,128]{2,0,1:T(8,128)S(1)} fusion(f32[3,256,128]{2,1,0:T(8,128)S(1)} %copy-done.2, s32[1024]{0:T(1024)S(1)} %broadcast_clamp_fusion.2), kind=kCustom, calls=%fused_computation.1 | custom fusion | bytes 3149824 | tf_op jit(solution)/shard_map/gather | solution.py:79
  34.1 15.0 %gather_fusion.3 = bf16[4096,128]{1,0:T(8,128)(2,1)} fusion(bf16[256,128]{1,0:T(8,128)(2,1)S(1)} %copy-done.1, s32[4096]{0:T(1024)S(1)} %broadcast_clamp_fusion), kind=kCustom, calls=%fused_computation.3 | custom fusion | bytes 2113536 | tf_op jit(solution)/shard_map/gather | solution.py:57
  49.2 6.7 %all-to-all-start.2 = ((bf16[16,64,4,128]{3,2,1,0:T(4,128)(2,1)}), bf16[16,64,4,128]{3,2,1,0:T(4,128)(2,1)}, u32[]{:S(2)}, u32[]{:S(2)}) async-start(bf16[16,64,4,128]{3,2,1,0:T(4,128)(2,1)} %bitcast.18), calls=%async_computation.2 | async-start | bytes 2097152 | tf_op jit(solution)/shard_map/all_to_all | solution.py:58
  55.9 68.3 %while.10 = (s32[]{:T(128)}, f32[16,16,128]{2,1,0:T(8,128)S(1)}, f32[16,16,4,128]{3,2,1,0:T(4,128)S(1)}, f32[16,3,16,128]{3,2,0,1:T(8,128)S(1)}, f32[16,3,16,4,128]{4,3,2,0,1:T(4,128)S(1)}, /*index=5*/s32[]{:T(128)}) while((s32[]{:T(128)}, f32[16,16,128]{2,1,0:T(8,128)S(1)}, f32[16,16,4,128]{3,2,1,0:T(4,128)S(1)}, ...), condition=%wide.region_3.4_spmd, body=%wide.region_0.3_spmd.sunk | while | flops 11532290 | bytes 8880221 | solution.py:82
  56.0 3.5 %multiply_reduce_fusion.4 = f32[16,4,128,128]{3,2,1,0:T(8,128)S(1)} fusion(f32[3,16,4,128]{3,2,1,0:T(4,128)S(1)} %dynamic-slice_bitcast_fusion.6, f32[3,16,128]{2,1,0:T(8,128)S(1)} %dynamic-slice_bitcast_fusion.7), kind=kLoop, calls=%fused_computation.5.clone.1 | loop fusion | flops 8388608 | bytes 4317184 | tf_op jit(solution)/shard_map/while/body/eval_jaxpr/reduce_sum | solution.py:18
  60.2 3.5 %multiply_reduce_fusion.4 = f32[16,4,128,128]{3,2,1,0:T(8,128)S(1)} fusion(f32[3,16,4,128]{3,2,1,0:T(4,128)S(1)} %dynamic-slice_bitcast_fusion.6, f32[3,16,128]{2,1,0:T(8,128)S(1)} %dynamic-slice_bitcast_fusion.7), kind=kLoop, calls=%fused_computation.5.clone.1 | loop fusion | flops 8388608 | bytes 4317184 | tf_op jit(solution)/shard_map/while/body/eval_jaxpr/reduce_sum | solution.py:18
  64.5 3.5 %multiply_reduce_fusion.4 = f32[16,4,128,128]{3,2,1,0:T(8,128)S(1)} fusion(f32[3,16,4,128]{3,2,1,0:T(4,128)S(1)} %dynamic-slice_bitcast_fusion.6, f32[3,16,128]{2,1,0:T(8,128)S(1)} %dynamic-slice_bitcast_fusion.7), kind=kLoop, calls=%fused_computation.5.clone.1 | loop fusion | flops 8388608 | bytes 4317184 | tf_op jit(solution)/shard_map/while/body/eval_jaxpr/reduce_sum | solution.py:18
  68.8 3.5 %multiply_reduce_fusion.4 = f32[16,4,128,128]{3,2,1,0:T(8,128)S(1)} fusion(f32[3,16,4,128]{3,2,1,0:T(4,128)S(1)} %dynamic-slice_bitcast_fusion.6, f32[3,16,128]{2,1,0:T(8,128)S(1)} %dynamic-slice_bitcast_fusion.7), kind=kLoop, calls=%fused_computation.5.clone.1 | loop fusion | flops 8388608 | bytes 4317184 | tf_op jit(solution)/shard_map/while/body/eval_jaxpr/reduce_sum | solution.py:18
  73.0 3.5 %multiply_reduce_fusion.4 = f32[16,4,128,128]{3,2,1,0:T(8,128)S(1)} fusion(f32[3,16,4,128]{3,2,1,0:T(4,128)S(1)} %dynamic-slice_bitcast_fusion.6, f32[3,16,128]{2,1,0:T(8,128)S(1)} %dynamic-slice_bitcast_fusion.7), kind=kLoop, calls=%fused_computation.5.clone.1 | loop fusion | flops 8388608 | bytes 4317184 | tf_op jit(solution)/shard_map/while/body/eval_jaxpr/reduce_sum | solution.py:18
  77.3 3.5 %multiply_reduce_fusion.4 = f32[16,4,128,128]{3,2,1,0:T(8,128)S(1)} fusion(f32[3,16,4,128]{3,2,1,0:T(4,128)S(1)} %dynamic-slice_bitcast_fusion.6, f32[3,16,128]{2,1,0:T(8,128)S(1)} %dynamic-slice_bitcast_fusion.7), kind=kLoop, calls=%fused_computation.5.clone.1 | loop fusion | flops 8388608 | bytes 4317184 | tf_op jit(solution)/shard_map/while/body/eval_jaxpr/reduce_sum | solution.py:18
  81.6 3.5 %multiply_reduce_fusion.4 = f32[16,4,128,128]{3,2,1,0:T(8,128)S(1)} fusion(f32[3,16,4,128]{3,2,1,0:T(4,128)S(1)} %dynamic-slice_bitcast_fusion.6, f32[3,16,128]{2,1,0:T(8,128)S(1)} %dynamic-slice_bitcast_fusion.7), kind=kLoop, calls=%fused_computation.5.clone.1 | loop fusion | flops 8388608 | bytes 4317184 | tf_op jit(solution)/shard_map/while/body/eval_jaxpr/reduce_sum | solution.py:18
  85.8 3.5 %multiply_reduce_fusion.4 = f32[16,4,128,128]{3,2,1,0:T(8,128)S(1)} fusion(f32[3,16,4,128]{3,2,1,0:T(4,128)S(1)} %dynamic-slice_bitcast_fusion.6, f32[3,16,128]{2,1,0:T(8,128)S(1)} %dynamic-slice_bitcast_fusion.7), kind=kLoop, calls=%fused_computation.5.clone.1 | loop fusion | flops 8388608 | bytes 4317184 | tf_op jit(solution)/shard_map/while/body/eval_jaxpr/reduce_sum | solution.py:18
  90.1 3.5 %multiply_reduce_fusion.4 = f32[16,4,128,128]{3,2,1,0:T(8,128)S(1)} fusion(f32[3,16,4,128]{3,2,1,0:T(4,128)S(1)} %dynamic-slice_bitcast_fusion.6, f32[3,16,128]{2,1,0:T(8,128)S(1)} %dynamic-slice_bitcast_fusion.7), kind=kLoop, calls=%fused_computation.5.clone.1 | loop fusion | flops 8388608 | bytes 4317184 | tf_op jit(solution)/shard_map/while/body/eval_jaxpr/reduce_sum | solution.py:18
  94.4 3.5 %multiply_reduce_fusion.4 = f32[16,4,128,128]{3,2,1,0:T(8,128)S(1)} fusion(f32[3,16,4,128]{3,2,1,0:T(4,128)S(1)} %dynamic-slice_bitcast_fusion.6, f32[3,16,128]{2,1,0:T(8,128)S(1)} %dynamic-slice_bitcast_fusion.7), kind=kLoop, calls=%fused_computation.5.clone.1 | loop fusion | flops 8388608 | bytes 4317184 | tf_op jit(solution)/shard_map/while/body/eval_jaxpr/reduce_sum | solution.py:18
  98.6 3.5 %multiply_reduce_fusion.4 = f32[16,4,128,128]{3,2,1,0:T(8,128)S(1)} fusion(f32[3,16,4,128]{3,2,1,0:T(4,128)S(1)} %dynamic-slice_bitcast_fusion.6, f32[3,16,128]{2,1,0:T(8,128)S(1)} %dynamic-slice_bitcast_fusion.7), kind=kLoop, calls=%fused_computation.5.clone.1 | loop fusion | flops 8388608 | bytes 4317184 | tf_op jit(solution)/shard_map/while/body/eval_jaxpr/reduce_sum | solution.py:18
  102.9 3.5 %multiply_reduce_fusion.4 = f32[16,4,128,128]{3,2,1,0:T(8,128)S(1)} fusion(f32[3,16,4,128]{3,2,1,0:T(4,128)S(1)} %dynamic-slice_bitcast_fusion.6, f32[3,16,128]{2,1,0:T(8,128)S(1)} %dynamic-slice_bitcast_fusion.7), kind=kLoop, calls=%fused_computation.5.clone.1 | loop fusion | flops 8388608 | bytes 4317184 | tf_op jit(solution)/shard_map/while/body/eval_jaxpr/reduce_sum | solution.py:18
  107.2 3.5 %multiply_reduce_fusion.4 = f32[16,4,128,128]{3,2,1,0:T(8,128)S(1)} fusion(f32[3,16,4,128]{3,2,1,0:T(4,128)S(1)} %dynamic-slice_bitcast_fusion.6, f32[3,16,128]{2,1,0:T(8,128)S(1)} %dynamic-slice_bitcast_fusion.7), kind=kLoop, calls=%fused_computation.5.clone.1 | loop fusion | flops 8388608 | bytes 4317184 | tf_op jit(solution)/shard_map/while/body/eval_jaxpr/reduce_sum | solution.py:18
  111.4 3.5 %multiply_reduce_fusion.4 = f32[16,4,128,128]{3,2,1,0:T(8,128)S(1)} fusion(f32[3,16,4,128]{3,2,1,0:T(4,128)S(1)} %dynamic-slice_bitcast_fusion.6, f32[3,16,128]{2,1,0:T(8,128)S(1)} %dynamic-slice_bitcast_fusion.7), kind=kLoop, calls=%fused_computation.5.clone.1 | loop fusion | flops 8388608 | bytes 4317184 | tf_op jit(solution)/shard_map/while/body/eval_jaxpr/reduce_sum | solution.py:18
  115.7 3.5 %multiply_reduce_fusion.4 = f32[16,4,128,128]{3,2,1,0:T(8,128)S(1)} fusion(f32[3,16,4,128]{3,2,1,0:T(4,128)S(1)} %dynamic-slice_bitcast_fusion.6, f32[3,16,128]{2,1,0:T(8,128)S(1)} %dynamic-slice_bitcast_fusion.7), kind=kLoop, calls=%fused_computation.5.clone.1 | loop fusion | flops 8388608 | bytes 4317184 | tf_op jit(solution)/shard_map/while/body/eval_jaxpr/reduce_sum | solution.py:18
  120.0 3.5 %multiply_reduce_fusion.4 = f32[16,4,128,128]{3,2,1,0:T(8,128)S(1)} fusion(f32[3,16,4,128]{3,2,1,0:T(4,128)S(1)} %dynamic-slice_bitcast_fusion.6, f32[3,16,128]{2,1,0:T(8,128)S(1)} %dynamic-slice_bitcast_fusion.7), kind=kLoop, calls=%fused_computation.5.clone.1 | loop fusion | flops 8388608 | bytes 4317184 | tf_op jit(solution)/shard_map/while/body/eval_jaxpr/reduce_sum | solution.py:18
  127.3 6.1 %convolution_convert_fusion = bf16[1024,16,128]{2,1,0:T(8,128)(2,1)S(1)} fusion(bf16[1024,4,128]{2,1,0:T(4,128)(2,1)} %bitcast.19, s32[1024,4]{1,0:T(8,128)S(1)} %bitcast.58), kind=kOutput, calls=%fused_computation.13 | convolution fusion | flops 18939904 | bytes 5259264 | tf_op jit(solution)/shard_map/nkp,nkc->npc/dot_general | solution.py:11
  133.4 1.3 fusion.2
  134.7 7.0 %gather_fusion.2 = bf16[2048,128]{1,0:T(8,128)(2,1)S(1)} fusion(bf16[4096,128]{1,0:T(8,128)(2,1)} %all-gather.2.cloned.1.call-done, s32[2048]{0:T(1024)S(1)} %broadcast_clamp_fusion.1), kind=kCustom, calls=%fused_computation.2 | custom fusion | bytes 1056768 | tf_op jit(solution)/shard_map/gather | solution.py:49
  141.7 1.1 convolution_convert_fusion.1
  143.2 6.1 %scatter_fusion = f32[256,128]{1,0:T(8,128)S(1)} fusion(f32[256,128]{1,0:T(8,128)S(1)} %convolution_bitcast_fusion, s32[1024]{0:T(1024)S(1)} %reshape.133, f32[1024,128]{1,0:T(8,128)S(1)} %fusion.2), kind=kCustom, calls=%fused_computation.4 | custom fusion | flops 131072 | bytes 1576960 | tf_op jit(solution)/shard_map/scatter-add | solution.py:67
  (124 shorter events, 18.7 us)
Async XLA Ops:
  6.5 126.9 %copy-start = (bf16[16,128,128]{2,1,0:T(8,128)(2,1)S(1)}, bf16[16,128,128]{2,1,0:T(8,128)(2,1)}, u32[]{:S(2)}) copy-start(bf16[16,128,128]{2,1,0:T(8,128)(2,1)} %param.18) | copy-start | bytes 1572868
  6.5 23.7 %copy-start.2 = (f32[3,256,128]{2,1,0:T(8,128)S(1)}, f32[3,256,128]{2,1,0:T(8,128)}, u32[]{:S(2)}) copy-start(f32[3,256,128]{2,1,0:T(8,128)} %param.16) | copy-start | bytes 1179652
  6.5 128.1 %all-gather.2.cloned.1.call-start = ((), (), s32[]{:S(2)}) async-start(), calls=%async_computation.3 | async-start | bytes 1114112 | tf_op jit(solution)/shard_map/all_gather | solution.py:48
  8.4 13.9 %all-to-all-start = ((s32[16,1,64]{2,1,0:T(1,128)}), s32[16,1,64]{2,1,0:T(1,128)S(1)}, u32[]{:S(2)}, u32[]{:S(2)}) async-start(s32[16,1,64]{2,1,0:T(1,128)} %bitcast.63), calls=%async_computation | async-start | bytes 16384 | tf_op jit(solution)/shard_map/all_to_all | solution.py:60
  22.3 26.9 %all-to-all-start.1 = ((s32[16,1,256]{2,1,0:T(1,128)}), s32[16,1,256]{2,1,0:T(1,128)S(1)}, u32[]{:S(2)}, u32[]{:S(2)}) async-start(s32[16,1,256]{2,1,0:T(1,128)} %reshape.153), calls=%async_computation.1 | async-start | bytes 32768 | tf_op jit(solution)/shard_map/all_to_all | solution.py:59
  30.2 3.9 %copy-start.1 = (bf16[256,128]{1,0:T(8,128)(2,1)S(1)}, bf16[256,128]{1,0:T(8,128)(2,1)}, u32[]{:S(2)}) copy-start(bf16[256,128]{1,0:T(8,128)(2,1)} %convolution_convert_fusion.2) | copy-start | bytes 196612
  49.2 78.1 %all-to-all-start.2 = ((bf16[16,64,4,128]{3,2,1,0:T(4,128)(2,1)}), bf16[16,64,4,128]{3,2,1,0:T(4,128)(2,1)}, u32[]{:S(2)}, u32[]{:S(2)}) async-start(bf16[16,64,4,128]{3,2,1,0:T(4,128)(2,1)} %bitcast.18), calls=%async_computation.2 | async-start | bytes 2097152 | tf_op jit(solution)/shard_map/all_to_all | solution.py:58
  55.9 68.3 %copy-start.5 = (s32[256,8]{0,1:T(8,128)S(1)}, s32[256,8]{0,1:T(8,128)}, u32[]{:S(2)}) copy-start(s32[256,8]{0,1:T(8,128)} %param.21) | copy-start | bytes 24580
  55.9 68.6 %copy-start.4 = (s32[256,8]{0,1:T(8,128)S(1)}, s32[256,8]{0,1:T(8,128)}, u32[]{:S(2)}) copy-start(s32[256,8]{0,1:T(8,128)} %param.22) | copy-start | bytes 24580
  143.1 6.1 %copy-start.3 = (bf16[128,128]{1,0:T(8,128)(2,1)S(1)}, bf16[128,128]{1,0:T(8,128)(2,1)}, u32[]{:S(2)}) copy-start(bf16[128,128]{1,0:T(8,128)(2,1)} %param.19) | copy-start | bytes 98308
  143.2 6.1 %copy-start.6 = (s32[256]{0:T(256)S(1)}, s32[256]{0:T(256)}, u32[]{:S(2)}) copy-start(s32[256]{0:T(256)} %param.15) | copy-start | bytes 3076
Sparse Core Ops, SparseCore 0:
  9.2 42.8 all-gather.1
where the time goes:
time: 158 us; the launch traced here: 157 us
  other arithmetic  75.1 us (48%)
  local copies, waits for them, and re-layouts  34.9 us (22%)
  starting transfers between devices  19.4 us (12%)
  between operations  13.7 us (9%)
  matrix products  11.4 us (7%)
  waiting for transfers between devices  1.62 us (1%)
    reduce_sum x16, other arithmetic, near_block(): dist_sq = jnp.sum(diffs * diffs, axis=0) + 0.0025  55.8 us
    gather x1, local copies, waits for them, and re-layouts, body(): rows = multipole[sources.reshape(-1)].reshape(groups, slots, fanin, width)  15 us
    reduce_sum x16, other arithmetic, near_block(): return jnp.sum(kernel, axis=(1, 3))  10.9 us
    all_to_all x1, starting transfers between devices, body(): lax.all_to_all(targets, 'oct', split_axis=0, concat_axis=0, tiled=True)  7.6 us
    dot_general x2, matrix products, pattern_sums(): jnp.einsum('nkp,nkc->npc', onehot, rows, preferred_element_type=jnp.float32)  7.14 us
    gather x1, local copies, waits for them, and re-layouts, body(): group_all[group_sources]  6.96 us
    all_to_all x1, starting transfers between devices, body(): lax.all_to_all(rows, 'oct', split_axis=0, concat_axis=0, tiled=True)  6.71 us
    scatter-add x1, other arithmetic, body(): jax.ops.segment_sum(received.reshape(-1, width), got_targets.reshape(-1),...  6.1 us
  transfers between devices with their start and end apart: 4, of which 1 were waited for; matrix products, arithmetic and copies ran while one was open for 66% of the time, Pallas kernels for 0%

commit v1 on v0

v1 whole, which is shorter than its diff:
```python
import functools
import math

import jax
import jax.numpy as jnp
from jax import lax
from jax.experimental import pallas as pl
from jax.experimental.pallas import tpu as pltpu
from jax.sharding import PartitionSpec as P

F32, BF16, I32 = jnp.float32, jnp.bfloat16, jnp.int32
MESH = pl.DeviceIdType.MESH
FEAT = 32
SOFT = 0.0025
NEAR_UNROLL = 32


def parts3(v):
    hi = v.astype(BF16).astype(F32)
    rest = v - hi
    mid = rest.astype(BF16).astype(F32)
    return hi, mid, rest - mid


def merge(a, b, first, shift, axis):
    return jnp.where(first, a, b) + pltpu.roll(jnp.where(first, b, a), shift, axis)


def column(row):
    return jnp.broadcast_to(row, (128, 128)).T


def build_features(p_ref, src_b, tgt_b, sub, unroll):
    is3, is7, lo3, lo4 = sub == 3, sub == 7, sub < 3, sub < 4
    pad = is3 | is7
    zero = jnp.zeros((8, 128), F32)

    def some(ii, carry):
        for bu in range(unroll):
            i = ii * unroll + bu
            cols = []
            for u in range(4):
                t = 4 * i + u
                v = jnp.where(pad, 0.0, p_ref[t] - 1.0)
                s = v * v
                s = s + pltpu.roll(s, 1, 0)
                n = s + pltpu.roll(s, 2, 0)
                w1, w2, w3 = parts3(jnp.where(pad, n, v))
                s0 = jnp.where(is7, 1.0, w1)
                s1 = jnp.where(is7, 1.0, w2)
                s2 = jnp.where(is7, 1.0, jnp.where(lo3, w1, w3))
                src_b[t] = jnp.concatenate([s0, s1, s2, zero], axis=0).astype(BF16)
                m1, m2, m3 = parts3(n + SOFT)
                y1, y2, y3 = -2.0 * w1, -2.0 * w2, -2.0 * w3
                base = jnp.where(is3, 1.0, jnp.where(lo4, y1, y2))
                t0 = jnp.where(is7, m1, base)
                t1 = jnp.where(is7, m2, base)
                t2 = jnp.where(is7, m3, jnp.where(is3, 1.0, jnp.where(lo4, y3, y1)))
                cols += [t0, t1, t2, zero]
            tgt_b[i] = jnp.concatenate(cols, axis=0).T.astype(BF16)
        return carry

    lax.fori_loop(0, src_b.shape[0] // (4 * unroll), some, 0)


def near_boxes_step(i, nb_ref, q_ref, src_b, tgt_b, near_ref, lane, sub):
    t0 = pl.multiple_of(NEAR_UNROLL * i, NEAR_UNROLL)
    knear = nb_ref.shape[0]
    rows = []
    for u in range(NEAR_UNROLL):
        lhs = tgt_b[(NEAR_UNROLL // 4) * i + u // 4]
        lo = FEAT * (u % 4)
        acc = None
        for pair in range(knear // 2):
            ids = [nb_ref[2 * pair + e, t0 + u] for e in range(2)]
            parts = [jnp.concatenate([src_b[s] for s in ids], axis=1)]
            if lo:
                parts.insert(0, jnp.zeros((lo, 256), BF16))
            if lo + FEAT < 128:
                parts.append(jnp.zeros((128 - FEAT - lo, 256), BF16))
            rhs = jnp.concatenate(parts, axis=0)
            inv = lax.rsqrt(jnp.dot(lhs, rhs, preferred_element_type=F32))
            for e in range(2):
                q = q_ref[pl.ds(ids[e], 1), :]
                term = inv[:, 128 * e : 128 * e + 128] * q
                acc = term if acc is None else acc + term
        row = None
        for g in range(16):
            total = jnp.sum(acc[8 * g : 8 * g + 8], axis=1, keepdims=True)
            x = jnp.where(lane == sub + 8 * g, total, 0.0)
            row = x if row is None else row + x
        rows.append(row)
    for b in range(NEAR_UNROLL // 8):
        some = rows[8 * b : 8 * b + 8]
        shift = 1
        while len(some) > 1:
            first = (sub & shift) == 0
            some = [merge(some[2 * n], some[2 * n + 1], first, shift, 0) for n in range(len(some) // 2)]
            shift *= 2
        near_ref[pl.ds(t0 + 8 * b, 8), :] = some[0]


def step_kernel(
    n_oct,
    n_cube,
    nb_ref,
    gs_ref,
    pos_ref,
    charges_ref,
    counts_ref,
    moment_ref,
    trans_ref,
    eval_ref,
    gp_ref,
    rs_ref,
    rp_ref,
    rt_ref,
    out_ref,
    p_ref,
    src_b,
    tgt_b,
    q_ref,
    near_ref,
    count_b,
    pat_b,
    gall,
    gf_ref,
    table,
    key_v,
    key_s,
    slot_f,
    msg,
    got,
    rows_ref,
    sums_ref,
    pos_sem,
    key_sem,
    right_send,
    right_recv,
    left_send,
    left_recv,
    sib_send,
    sib_recv,
    oct_send,
    oct_recv,
):
    o = lax.axis_index("oct")
    c = lax.axis_index("cube")
    boxes, panels = charges_ref.shape
    width = moment_ref.shape[1]
    n_pat = trans_ref.shape[0]
    klist = gs_ref.shape[0]
    fanin = rs_ref.shape[1]
    slots = rs_ref.shape[2]
    chips = n_cube // 2
    right = lax.rem(c + 2, n_cube)
    left = lax.rem(c + n_cube - 2, n_cube)
    sib = c + 1 - 2 * lax.rem(c, 2)

    barrier = pltpu.get_barrier_semaphore()
    for peer in (right, left, sib):
        pl.semaphore_signal(barrier, inc=1, device_id={"cube": peer}, device_id_type=MESH)
    for i in range(n_oct - 1):
        d = lax.rem(o + 1 + i, n_oct)
        pl.semaphore_signal(barrier, inc=1, device_id={"oct": d}, device_id_type=MESH)

    pos_copies = [
        pltpu.make_async_copy(pos_ref.at[d], p_ref.at[:, d + 4 * e], pos_sem.at[d + 3 * e])
        for d in range(3)
        for e in range(2)
    ]
    for copy in pos_copies:
        copy.start()

    key_v[...] = rp_ref[...] * boxes + rs_ref[...]
    key_copy = pltpu.make_async_copy(key_v, key_s, key_sem.at[0])
    key_copy.start()

    lane = lax.broadcasted_iota(I32, (8, 128), 1)
    sub = lax.broadcasted_iota(I32, (8, 128), 0)

    lane_big = lax.broadcasted_iota(I32, (128, 128), 1)
    for h in range(boxes // 128):
        half = slice(128 * h, 128 * h + 128)
        count_b[half] = column(counts_ref[h : h + 1, :])
        charge = charges_ref[half].astype(F32)
        q_ref[half] = jnp.where(lane_big < count_b[half], charge, 0.0)
    strength = q_ref[...].astype(BF16)
    multipole = jnp.dot(strength, moment_ref[...], preferred_element_type=F32).astype(BF16)
    gall[c] = multipole
    for p in range(n_pat):
        table[p * boxes : (p + 1) * boxes] = jnp.dot(
            multipole, trans_ref[p], preferred_element_type=F32
        )

    pl.semaphore_wait(barrier, 3 + n_oct - 1)

    def send(shard, peer, sends, recvs, n):
        return pltpu.make_async_remote_copy(
            src_ref=gall.at[shard],
            dst_ref=gall.at[shard],
            send_sem=sends.at[n],
            recv_sem=recvs.at[n],
            device_id={"cube": peer},
            device_id_type=MESH,
        )

    n_right = chips // 2
    n_left = chips - 1 - n_right
    from_left = [lax.rem(c + n_cube - 2 * h, n_cube) for h in range(n_right + 1)]
    from_right = [lax.rem(c + 2 * h, n_cube) for h in range(n_left + 1)]
    to_right = [send(from_left[h], right, right_send, right_recv, h) for h in range(n_right)]
    to_left = [send(from_right[h], left, left_send, left_recv, h) for h in range(n_left)]
    to_sib = [send(from_left[h], sib, sib_send, sib_recv, h) for h in range(n_right + 1)]
    to_sib += [
        send(from_right[h], sib, sib_send, sib_recv, n_right + h) for h in range(1, n_left + 1)
    ]

    to_right[0].start()
    to_left[0].start()
    to_sib[0].start()

    def ring_step(h):
        if h <= n_right:
            to_right[h - 1].wait_recv()
        if h <= n_left:
            to_left[h - 1].wait_recv()
        if h < n_right:
            to_right[h].start()
        if h < n_left:
            to_left[h].start()
        if h <= n_right:
            to_sib[h].start()
        if h <= n_left:
            to_sib[n_right + h].start()

    key_copy.wait()
    targets = rt_ref[...].astype(F32)
    blank = jnp.zeros_like(targets)
    odd = lax.rem(o, 2)
    target_rows = jnp.where(
        odd == 0,
        jnp.concatenate([targets, blank], axis=1),
        jnp.concatenate([blank, targets], axis=1),
    )
    for d in range(n_oct):
        msg[d, slots : slots + 16, :] = jnp.broadcast_to(
            target_rows[d : d + 1], (16, 2 * slots)
        ).astype(BF16)

    def fill(d):
        for j in range(slots):
            total = None
            for k in range(fanin):
                row = table[pl.ds(key_s[d, k, j], 1), :]
                total = row if total is None else total + row
            slot_f[j : j + 1, :] = total
        msg[d, 0:slots, :] = slot_f[...].astype(BF16)

    def to_oct(i):
        d = lax.rem(o + 1 + i, n_oct)
        return pltpu.make_async_remote_copy(
            src_ref=msg.at[d],
            dst_ref=got.at[o],
            send_sem=oct_send.at[i],
            recv_sem=oct_recv.at[i],
            device_id={"oct": d},
            device_id_type=MESH,
        )

    def one_group(i, carry):
        fill(lax.rem(o + 1 + i, n_oct))

        @pl.when(i < n_oct - 1)
        def _():
            to_oct(i).start()

        return carry

    lax.fori_loop(0, n_oct, one_group, 0)
    got[o] = msg[o]

    for copy in pos_copies:
        copy.wait()
    build_features(p_ref, src_b, tgt_b, sub, 8)
    for k in range(klist):
        for h in range(boxes // 128):
            pat_b[k, 128 * h : 128 * h + 128] = column(gp_ref[k : k + 1, 128 * h : 128 * h + 128])

    def near_step(i, carry):
        for h in range(1, n_right + 1):

            @pl.when(i == h)
            def _(h=h):
                ring_step(h)

        near_boxes_step(i, nb_ref, q_ref, src_b, tgt_b, near_ref, lane, sub)
        return carry

    lax.fori_loop(0, boxes // NEAR_UNROLL, near_step, 0)

    for copy in to_sib:
        copy.wait_recv()
    gf_ref[...] = gall[...].reshape(n_cube * boxes, width).astype(F32)

    def gather(i, carry):
        t0 = pl.multiple_of(16 * i, 16)
        for u in range(16):
            for k in range(klist):
                rows_ref[k, pl.ds(t0 + u, 1), :] = gf_ref[pl.ds(gs_ref[k, t0 + u], 1), :]
        return carry

    lax.fori_loop(0, boxes // 16, gather, 0)

    def pattern_sums(i, carry):
        t0 = pl.ds(pl.multiple_of(16 * i, 16), 16)
        pats = [pat_b[k, t0] for k in range(klist)]
        rows = [rows_ref[k, t0] for k in range(klist)]
        for p in range(n_pat):
            total = None
            for k in range(klist):
                x = jnp.where(pats[k] == p, rows[k], 0.0)
                total = x if total is None else total + x
            sums_ref[t0, p * width : (p + 1) * width] = total.astype(BF16)
        return carry

    lax.fori_loop(0, boxes // 16, pattern_sums, 0)
    operators = trans_ref[...].reshape(n_pat * width, width)
    local = jnp.dot(sums_ref[...], operators, preferred_element_type=F32)

    for i in range(n_oct - 1):
        to_oct(i).wait_recv()
    box = lax.broadcasted_iota(I32, (boxes, 2 * slots), 0).astype(F32)
    for m in range(n_oct // 4):
        hot, vals = [], []
        for e in (4 * m, 4 * m + 2):
            trow = got[e, slots : slots + 16, :].astype(F32) + got[
                e + 1, slots : slots + 16, :
            ].astype(F32)
            hot.append(jnp.where(box == trow[0:1], 1.0, 0.0).astype(BF16))
            vals += [got[e, 0:slots, :], got[e + 1, 0:slots, :]]
        local = local + jnp.dot(
            jnp.concatenate(hot, axis=1),
            jnp.concatenate(vals, axis=0),
            preferred_element_type=F32,
        )

    far = jnp.dot(local.astype(BF16), eval_ref[...], preferred_element_type=F32)
    total = near_ref[...] * (1.0 / (4.0 * math.pi)) + far
    panel = lax.broadcasted_iota(I32, (boxes, panels), 1)
    out_ref[...] = jnp.where(panel < count_b[...], total, 0.0)

    for copy in to_right + to_left + to_sib:
        copy.wait_send()
    for i in range(n_oct - 1):
        to_oct(i).wait_send()


def body(
    n_oct,
    n_cube,
    charges,
    panel_counts,
    positions,
    moment_map,
    translations,
    evaluation,
    near_boxes,
    group_sources,
    group_patterns,
    remote_sources,
    remote_patterns,
    remote_targets,
):
    boxes, panels = charges.shape
    width = moment_map.shape[1]
    n_pat = translations.shape[0]
    klist = group_sources.shape[1]
    slots, fanin = remote_sources.shape[3:]
    chips = n_cube // 2
    sources = remote_sources[0, 0].transpose(0, 2, 1)
    patterns = remote_patterns[0, 0].transpose(0, 2, 1)
    smem = pl.BlockSpec(memory_space=pltpu.SMEM)
    vmem = pl.BlockSpec(memory_space=pltpu.VMEM)
    dma = pltpu.SemaphoreType.DMA
    return pl.pallas_call(
        functools.partial(step_kernel, n_oct, n_cube),
        out_shape=jax.ShapeDtypeStruct((boxes, panels), F32),
        in_specs=[smem, smem, pl.BlockSpec(memory_space=pl.ANY)] + [vmem] * 9,
        out_specs=vmem,
        scratch_shapes=[
            pltpu.VMEM((boxes, 8, panels), F32),
            pltpu.VMEM((boxes, FEAT, panels), BF16),
            pltpu.VMEM((boxes // 4, panels, 4 * FEAT), BF16),
            pltpu.VMEM((boxes, panels), F32),
            pltpu.VMEM((boxes, panels), F32),
            pltpu.VMEM((boxes, panels), I32),
            pltpu.VMEM((klist, boxes, width), I32),
            pltpu.VMEM((n_cube, boxes, width), BF16),
            pltpu.VMEM((n_cube * boxes, width), F32),
            pltpu.VMEM((n_pat * boxes, width), F32),
            pltpu.VMEM((n_oct, fanin, slots), I32),
            pltpu.SMEM((n_oct, fanin, slots), I32),
            pltpu.VMEM((slots, width), F32),
            pltpu.VMEM((n_oct, slots + 16, width), BF16),
            pltpu.VMEM((n_oct, slots + 16, width), BF16),
            pltpu.VMEM((klist, boxes, width), F32),
            pltpu.VMEM((boxes, n_pat * width), BF16),
            dma((6,)),
            dma((1,)),
            dma((chips,)),
            dma((chips,)),
            dma((chips,)),
            dma((chips,)),
            dma((chips,)),
            dma((chips,)),
            dma((n_oct,)),
            dma((n_oct,)),
        ],
        compiler_params=pltpu.CompilerParams(
            collective_id=0, has_side_effects=True, vmem_limit_bytes=48 << 20
        ),
    )(
        near_boxes.T,
        group_sources.T,
        positions,
        charges,
        panel_counts.reshape(boxes // 128, 128),
        moment_map,
        translations,
        evaluation,
        group_patterns.T,
        sources,
        patterns,
        remote_targets[0, 0],
    )


def solution(mesh):
    n_oct, n_cube = mesh.shape["oct"], mesh.shape["cube"]
    return jax.shard_map(
        functools.partial(body, n_oct, n_cube),
        mesh=mesh,
        in_specs=(
            P(("oct", "cube"), None),
            P(("oct", "cube")),
            P(None, ("oct", "cube"), None),
            P(),
            P(),
            P(),
            P(("oct", "cube"), None),
            P(("oct", "cube"), None),
            P(("oct", "cube"), None),
            P("oct", "cube", None, None, None),
            P("oct", "cube", None, None, None),
            P("oct", "cube", None, None),
        ),
        out_specs=P(("oct", "cube"), None),
        check_vma=False,
    )
```

time: 158 us -> 50.2 us (0.32)
  the two profiles are of different devices: /device:TPU:1 before, /device:TPU:8 now
where the time goes in v1:
time: 50.2 us; the launch traced here: 49.6 us
  Pallas kernels  40.9 us (81%)
  local copies, waits for them, and re-layouts  8.66 us (17%)
    pallas_call x1, Pallas kernels, body(): pl.pallas_call(functools.partial(step_kernel, n_oct, n_cube), out_shape=j...  40.9 us
    unnamed x25, local copies, waits for them, and re-layouts  8.66 us

profile of v1, /device:TPU:8, one launch (start us, length us, event | category | flops | bytes accessed | tf_op | source)
XLA Modules:
  0.0 49.6 jit_solution(15788492357708322794)
XLA Ops:
  0.0 0.0 copy-start.7
  0.0 0.0 copy-start.10
  0.0 0.0 copy-start.11
  0.0 0.7 %copy-done.7 = s32[256,8]{0,1:T(8,128)S(1)} copy-done((s32[256,8]{0,1:T(8,128)S(1)}, s32[256,8]{0,1:T(8,128)}, u32[]{:S(2)}) %copy-start.7) | copy-done | bytes 8216
  0.7 0.0 copy-done.10
  0.7 0.0 copy-done.11
  0.7 0.0 copy-start
  0.7 1.0 %copy-done = bf16[16,128,128]{2,1,0:T(8,128)(2,1)S(1)} copy-done((bf16[16,128,128]{2,1,0:T(8,128)(2,1)S(1)}, bf16[16,128,128]{2,1,0:T(8,128)(2,1)}, u32[]{:S(2)}) %copy-start) | copy-done | bytes 524312
  1.8 0.0 copy-start.1
  1.8 1.0 %copy-done.1 = f32[3,256,128]{2,1,0:T(8,128)S(1)} copy-done((f32[3,256,128]{2,1,0:T(8,128)S(1)}, f32[3,256,128]{2,1,0:T(8,128)}, u32[]{:S(2)}) %copy-start.1) | copy-done | bytes 393240
  2.8 0.0 copy-start.2
  2.8 0.8 %copy-done.2 = bf16[256,128]{1,0:T(8,128)(2,1)S(1)} copy-done((bf16[256,128]{1,0:T(8,128)(2,1)S(1)}, bf16[256,128]{1,0:T(8,128)(2,1)}, u32[]{:S(2)}) %copy-start.2) | copy-done | bytes 65560
  3.6 0.0 copy-start.3
  3.6 0.8 %copy-done.3 = bf16[128,128]{1,0:T(8,128)(2,1)S(1)} copy-done((bf16[128,128]{1,0:T(8,128)(2,1)S(1)}, bf16[128,128]{1,0:T(8,128)(2,1)}, u32[]{:S(2)}) %copy-start.3) | copy-done | bytes 32792
  4.3 0.0 copy-start.4
  4.4 0.8 %copy-done.4 = bf16[128,128]{1,0:T(8,128)(2,1)S(1)} copy-done((bf16[128,128]{1,0:T(8,128)(2,1)S(1)}, bf16[128,128]{1,0:T(8,128)(2,1)}, u32[]{:S(2)}) %copy-start.4) | copy-done | bytes 32792
  5.1 0.0 copy-start.5
  5.1 0.8 %copy-done.5 = s32[1,1,16,64,4]{3,4,2,1,0:T(4,128)S(1)} copy-done((s32[1,1,16,64,4]{3,4,2,1,0:T(4,128)S(1)}, s32[1,1,16,64,4]{3,4,2,1,0:T(4,128)}, u32[]{:S(2)}) %copy-start.5) | copy-done | bytes 16408
  5.9 0.0 copy-start.6
  5.9 0.8 %copy-done.6 = s32[1,1,16,64,4]{3,4,2,1,0:T(4,128)S(1)} copy-done((s32[1,1,16,64,4]{3,4,2,1,0:T(4,128)S(1)}, s32[1,1,16,64,4]{3,4,2,1,0:T(4,128)}, u32[]{:S(2)}) %copy-start.6) | copy-done | bytes 16408
  6.6 0.0 copy-start.8
  6.6 0.7 %copy-done.8 = s32[256,8]{0,1:T(8,128)S(1)} copy-done((s32[256,8]{0,1:T(8,128)S(1)}, s32[256,8]{0,1:T(8,128)}, u32[]{:S(2)}) %copy-start.8) | copy-done | bytes 8216
  7.3 0.0 copy-start.9
  7.3 0.7 %copy-done.9 = s32[1,1,16,64]{3,2,1,0:T(8,128)S(1)} copy-done((s32[1,1,16,64]{3,2,1,0:T(8,128)S(1)}, s32[1,1,16,64]{3,2,1,0:T(8,128)}, u32[]{:S(2)}) %copy-start.9) | copy-done | bytes 4120
  8.0 40.9 %shard_map.118 = f32[256,128]{1,0:T(8,128)S(1)} custom-call(s32[4,256]{1,0:T(4,128)S(1)} %bitcast.16, s32[8,256]{1,0:T(8,128)S(1)} %bitcast.13, f32[3,256,128]{2,1,0:T(8,128)S(1)} %copy-done.1, bf16[256,128]{1,0:T(8,128)(2,1)S(1)} %copy-done.2, s32[2,128]{1,0:T(2,128)S(1)} %bitcast.17, bf16[128,128]{1,0:T(8,128)(2,1)S(1)} %copy-done.3, ...), custom_call_target="tpu_custom_call" | custom-call | tf_op jit(solution)/shard_map/pallas_call | solution.py:386
  48.9 0.7 %copy.14 = f32[256,128]{1,0:T(8,128)} copy(f32[256,128]{1,0:T(8,128)S(1)} %shard_map.118) | data formatting | bytes 262144
Async XLA Ops:
  0.0 0.7 %copy-start.7 = (s32[256,8]{0,1:T(8,128)S(1)}, s32[256,8]{0,1:T(8,128)}, u32[]{:S(2)}) copy-start(s32[256,8]{0,1:T(8,128)} %param.19) | copy-start | bytes 24580
  0.0 0.7 %copy-start.10 = (s32[256,4]{0,1:T(4,128)S(1)}, s32[256,4]{0,1:T(4,128)}, u32[]{:S(2)}) copy-start(s32[256,4]{0,1:T(4,128)} %param.18) | copy-start | bytes 12292
  0.0 0.7 %copy-start.11 = (s32[256]{0:T(256)S(1)}, s32[256]{0:T(256)}, u32[]{:S(2)}) copy-start(s32[256]{0:T(256)} %param.13) | copy-start | bytes 3076
  0.7 1.0 %copy-start = (bf16[16,128,128]{2,1,0:T(8,128)(2,1)S(1)}, bf16[16,128,128]{2,1,0:T(8,128)(2,1)}, u32[]{:S(2)}) copy-start(bf16[16,128,128]{2,1,0:T(8,128)(2,1)} %trans_ref.1) | copy-start | bytes 1572868
  1.8 1.0 %copy-start.1 = (f32[3,256,128]{2,1,0:T(8,128)S(1)}, f32[3,256,128]{2,1,0:T(8,128)}, u32[]{:S(2)}) copy-start(f32[3,256,128]{2,1,0:T(8,128)} %pos_ref.1) | copy-start | bytes 1179652
  2.8 0.8 %copy-start.2 = (bf16[256,128]{1,0:T(8,128)(2,1)S(1)}, bf16[256,128]{1,0:T(8,128)(2,1)}, u32[]{:S(2)}) copy-start(bf16[256,128]{1,0:T(8,128)(2,1)} %charges_ref.1) | copy-start | bytes 196612
  3.6 0.8 %copy-start.3 = (bf16[128,128]{1,0:T(8,128)(2,1)S(1)}, bf16[128,128]{1,0:T(8,128)(2,1)}, u32[]{:S(2)}) copy-start(bf16[128,128]{1,0:T(8,128)(2,1)} %moment_ref.1) | copy-start | bytes 98308
  4.3 0.8 %copy-start.4 = (bf16[128,128]{1,0:T(8,128)(2,1)S(1)}, bf16[128,128]{1,0:T(8,128)(2,1)}, u32[]{:S(2)}) copy-start(bf16[128,128]{1,0:T(8,128)(2,1)} %eval_ref.1) | copy-start | bytes 98308
  5.1 0.8 %copy-start.5 = (s32[1,1,16,64,4]{3,4,2,1,0:T(4,128)S(1)}, s32[1,1,16,64,4]{3,4,2,1,0:T(4,128)}, u32[]{:S(2)}) copy-start(s32[1,1,16,64,4]{3,4,2,1,0:T(4,128)} %param.21) | copy-start | bytes 49156
  5.9 0.8 %copy-start.6 = (s32[1,1,16,64,4]{3,4,2,1,0:T(4,128)S(1)}, s32[1,1,16,64,4]{3,4,2,1,0:T(4,128)}, u32[]{:S(2)}) copy-start(s32[1,1,16,64,4]{3,4,2,1,0:T(4,128)} %param.22) | copy-start | bytes 49156
  6.6 0.7 %copy-start.8 = (s32[256,8]{0,1:T(8,128)S(1)}, s32[256,8]{0,1:T(8,128)}, u32[]{:S(2)}) copy-start(s32[256,8]{0,1:T(8,128)} %param.20) | copy-start | bytes 24580
  7.3 0.7 %copy-start.9 = (s32[1,1,16,64]{3,2,1,0:T(8,128)S(1)}, s32[1,1,16,64]{3,2,1,0:T(8,128)}, u32[]{:S(2)}) copy-start(s32[1,1,16,64]{3,2,1,0:T(8,128)} %param.23) | copy-start | bytes 12292

commit v2 on v1

--- a/solution.py
+++ b/solution.py
@@ -13,6 +13,7 @@
 FEAT = 32
 SOFT = 0.0025
 NEAR_UNROLL = 32
+RING_FROM = 2
 
 
 def parts3(v):
@@ -30,37 +31,30 @@
     return jnp.broadcast_to(row, (128, 128)).T
 
 
-def build_features(p_ref, src_b, tgt_b, sub, unroll):
+def features_of_four(i, p_ref, src_b, tgt_b, sub):
     is3, is7, lo3, lo4 = sub == 3, sub == 7, sub < 3, sub < 4
     pad = is3 | is7
     zero = jnp.zeros((8, 128), F32)
-
-    def some(ii, carry):
-        for bu in range(unroll):
-            i = ii * unroll + bu
-            cols = []
-            for u in range(4):
-                t = 4 * i + u
-                v = jnp.where(pad, 0.0, p_ref[t] - 1.0)
-                s = v * v
-                s = s + pltpu.roll(s, 1, 0)
-                n = s + pltpu.roll(s, 2, 0)
-                w1, w2, w3 = parts3(jnp.where(pad, n, v))
-                s0 = jnp.where(is7, 1.0, w1)
-                s1 = jnp.where(is7, 1.0, w2)
-                s2 = jnp.where(is7, 1.0, jnp.where(lo3, w1, w3))
-                src_b[t] = jnp.concatenate([s0, s1, s2, zero], axis=0).astype(BF16)
-                m1, m2, m3 = parts3(n + SOFT)
-                y1, y2, y3 = -2.0 * w1, -2.0 * w2, -2.0 * w3
-                base = jnp.where(is3, 1.0, jnp.where(lo4, y1, y2))
-                t0 = jnp.where(is7, m1, base)
-                t1 = jnp.where(is7, m2, base)
-                t2 = jnp.where(is7, m3, jnp.where(is3, 1.0, jnp.where(lo4, y3, y1)))
-                cols += [t0, t1, t2, zero]
-            tgt_b[i] = jnp.concatenate(cols, axis=0).T.astype(BF16)
-        return carry
-
-    lax.fori_loop(0, src_b.shape[0] // (4 * unroll), some, 0)
+    cols = []
+    for u in range(4):
+        t = 4 * i + u
+        v = jnp.where(pad, 0.0, p_ref[t] - 1.0)
+        s = v * v
+        s = s + pltpu.roll(s, 1, 0)
+        n = s + pltpu.roll(s, 2, 0)
+        w1, w2, w3 = parts3(jnp.where(pad, n, v))
+        s0 = jnp.where(is7, 1.0, w1)
+        s1 = jnp.where(is7, 1.0, w2)
+        s2 = jnp.where(is7, 1.0, jnp.where(lo3, w1, w3))
+        src_b[t] = jnp.concatenate([s0, s1, s2, zero], axis=0).astype(BF16)
+        m1, m2, m3 = parts3(n + SOFT)
+        y1, y2, y3 = -2.0 * w1, -2.0 * w2, -2.0 * w3
+        base = jnp.where(is3, 1.0, jnp.where(lo4, y1, y2))
+        t0 = jnp.where(is7, m1, base)
+        t1 = jnp.where(is7, m2, base)
+        t2 = jnp.where(is7, m3, jnp.where(is3, 1.0, jnp.where(lo4, y3, y1)))
+        cols += [t0, t1, t2, zero]
+    tgt_b[i] = jnp.concatenate(cols, axis=0).T.astype(BF16)
 
 
 def near_boxes_step(i, nb_ref, q_ref, src_b, tgt_b, near_ref, lane, sub):
@@ -103,19 +97,30 @@
 def step_kernel(
     n_oct,
     n_cube,
-    nb_ref,
-    gs_ref,
     pos_ref,
+    charges_in,
+    counts_in,
+    moment_in,
+    trans_in,
+    rs_in,
+    rp_in,
+    nb_in,
+    rt_in,
+    gs_in,
+    gp_in,
+    eval_in,
+    out_ref,
     charges_ref,
     counts_ref,
     moment_ref,
     trans_ref,
-    eval_ref,
-    gp_ref,
     rs_ref,
     rp_ref,
+    nb_ref,
     rt_ref,
-    out_ref,
+    gs_ref,
+    gp_ref,
+    eval_ref,
     p_ref,
     src_b,
     tgt_b,
@@ -133,6 +138,7 @@
     got,
     rows_ref,
     sums_ref,
+    in_sem,
     pos_sem,
     key_sem,
     right_send,
@@ -157,6 +163,28 @@
     left = lax.rem(c + n_cube - 2, n_cube)
     sib = c + 1 - 2 * lax.rem(c, 2)
 
+    pairs = (
+        (charges_in, charges_ref),
+        (counts_in, counts_ref),
+        (moment_in, moment_ref),
+        (rs_in, rs_ref),
+        (rp_in, rp_ref),
+        (trans_in, trans_ref),
+        (nb_in, nb_ref),
+        (rt_in, rt_ref),
+        (gs_in, gs_ref),
+        (gp_in, gp_ref),
+        (eval_in, eval_ref),
+    )
+    copies = [pltpu.make_async_copy(a, b, in_sem.at[i]) for i, (a, b) in enumerate(pairs)]
+    pos_copies = [
+        pltpu.make_async_copy(pos_ref.at[d], p_ref.at[:, d + 4 * e], pos_sem.at[d + 3 * e])
+        for d in range(3)
+        for e in range(2)
+    ]
+    for copy in copies[:5] + pos_copies + copies[5:]:
+        copy.start()
+
     barrier = pltpu.get_barrier_semaphore()
     for peer in (right, left, sib):
         pl.semaphore_signal(barrier, inc=1, device_id={"cube": peer}, device_id_type=MESH)
@@ -164,21 +192,14 @@
         d = lax.rem(o + 1 + i, n_oct)
         pl.semaphore_signal(barrier, inc=1, device_id={"oct": d}, device_id_type=MESH)
 
-    pos_copies = [
-        pltpu.make_async_copy(pos_ref.at[d], p_ref.at[:, d + 4 * e], pos_sem.at[d + 3 * e])
-        for d in range(3)
-        for e in range(2)
-    ]
-    for copy in pos_copies:
-        copy.start()
-
+    lane = lax.broadcasted_iota(I32, (8, 128), 1)
+    sub = lax.broadcasted_iota(I32, (8, 128), 0)
+
+    for copy in copies[:5]:
+        copy.wait()
     key_v[...] = rp_ref[...] * boxes + rs_ref[...]
     key_copy = pltpu.make_async_copy(key_v, key_s, key_sem.at[0])
     key_copy.start()
-
-    lane = lax.broadcasted_iota(I32, (8, 128), 1)
-    sub = lax.broadcasted_iota(I32, (8, 128), 0)
-
     lane_big = lax.broadcasted_iota(I32, (128, 128), 1)
     for h in range(boxes // 128):
         half = slice(128 * h, 128 * h + 128)
@@ -188,10 +209,46 @@
     strength = q_ref[...].astype(BF16)
     multipole = jnp.dot(strength, moment_ref[...], preferred_element_type=F32).astype(BF16)
     gall[c] = multipole
+    for copy in copies[5:]:
+        copy.wait()
     for p in range(n_pat):
         table[p * boxes : (p + 1) * boxes] = jnp.dot(
             multipole, trans_ref[p], preferred_element_type=F32
         )
+    for copy in pos_copies:
+        copy.wait()
+
+    targets = rt_ref[...].astype(F32)
+    blank = jnp.zeros_like(targets)
+    odd = lax.rem(o, 2)
+    target_rows = jnp.where(
+        odd == 0,
+        jnp.concatenate([targets, blank], axis=1),
+        jnp.concatenate([blank, targets], axis=1),
+    )
+    for d in range(n_oct):
+        msg[d, slots : slots + 16, :] = jnp.broadcast_to(
+            target_rows[d : d + 1], (16, 2 * slots)
+        ).astype(BF16)
+    key_copy.wait()
+    groups_each = boxes // (4 * n_oct)
+
+    def one_group(d, carry):
+        for j in range(slots):
+            total = None
+            for k in range(fanin):
+                row = table[pl.ds(key_s[d, k, j], 1), :]
+                total = row if total is None else total + row
+            slot_f[j : j + 1, :] = total
+        for u in range(groups_each):
+            features_of_four(d * groups_each + u, p_ref, src_b, tgt_b, sub)
+        msg[d, 0:slots, :] = slot_f[...].astype(BF16)
+        return carry
+
+    lax.fori_loop(0, n_oct, one_group, 0)
+    for k in range(klist):
+        for h in range(boxes // 128):
+            pat_b[k, 128 * h : 128 * h + 128] = column(gp_ref[k : k + 1, 128 * h : 128 * h + 128])
 
     pl.semaphore_wait(barrier, 3 + n_oct - 1)
 
@@ -234,29 +291,6 @@
         if h <= n_left:
             to_sib[n_right + h].start()
 
-    key_copy.wait()
-    targets = rt_ref[...].astype(F32)
-    blank = jnp.zeros_like(targets)
-    odd = lax.rem(o, 2)
-    target_rows = jnp.where(
-        odd == 0,
-        jnp.concatenate([targets, blank], axis=1),
-        jnp.concatenate([blank, targets], axis=1),
-    )
-    for d in range(n_oct):
-        msg[d, slots : slots + 16, :] = jnp.broadcast_to(
-            target_rows[d : d + 1], (16, 2 * slots)
-        ).astype(BF16)
-
-    def fill(d):
-        for j in range(slots):
-            total = None
-            for k in range(fanin):
-                row = table[pl.ds(key_s[d, k, j], 1), :]
-                total = row if total is None else total + row
-            slot_f[j : j + 1, :] = total
-        msg[d, 0:slots, :] = slot_f[...].astype(BF16)
-
     def to_oct(i):
         d = lax.rem(o + 1 + i, n_oct)
         return pltpu.make_async_remote_copy(
@@ -268,29 +302,14 @@
             device_id_type=MESH,
         )
 
-    def one_group(i, carry):
-        fill(lax.rem(o + 1 + i, n_oct))
-
-        @pl.when(i < n_oct - 1)
-        def _():
-            to_oct(i).start()
-
-        return carry
-
-    lax.fori_loop(0, n_oct, one_group, 0)
+    for i in range(n_oct - 1):
+        to_oct(i).start()
     got[o] = msg[o]
-
-    for copy in pos_copies:
-        copy.wait()
-    build_features(p_ref, src_b, tgt_b, sub, 8)
-    for k in range(klist):
-        for h in range(boxes // 128):
-            pat_b[k, 128 * h : 128 * h + 128] = column(gp_ref[k : k + 1, 128 * h : 128 * h + 128])
 
     def near_step(i, carry):
         for h in range(1, n_right + 1):
 
-            @pl.when(i == h)
+            @pl.when(i == h + RING_FROM)
             def _(h=h):
                 ring_step(h)
 
@@ -380,15 +399,24 @@
     chips = n_cube // 2
     sources = remote_sources[0, 0].transpose(0, 2, 1)
     patterns = remote_patterns[0, 0].transpose(0, 2, 1)
-    smem = pl.BlockSpec(memory_space=pltpu.SMEM)
-    vmem = pl.BlockSpec(memory_space=pltpu.VMEM)
     dma = pltpu.SemaphoreType.DMA
     return pl.pallas_call(
         functools.partial(step_kernel, n_oct, n_cube),
         out_shape=jax.ShapeDtypeStruct((boxes, panels), F32),
-        in_specs=[smem, smem, pl.BlockSpec(memory_space=pl.ANY)] + [vmem] * 9,
-        out_specs=vmem,
+        in_specs=[pl.BlockSpec(memory_space=pltpu.HBM)] * 12,
+        out_specs=pl.BlockSpec(memory_space=pltpu.VMEM),
         scratch_shapes=[
+            pltpu.VMEM((boxes, panels), BF16),
+            pltpu.VMEM((boxes // 128, 128), I32),
+            pltpu.VMEM((panels, width), BF16),
+            pltpu.VMEM((n_pat, width, width), BF16),
+            pltpu.VMEM((n_oct, fanin, slots), I32),
+            pltpu.VMEM((n_oct, fanin, slots), I32),
+            pltpu.SMEM((near_boxes.shape[1], boxes), I32),
+            pltpu.VMEM((n_oct, slots), I32),
+            pltpu.SMEM((klist, boxes), I32),
+            pltpu.VMEM((klist, boxes), I32),
+            pltpu.VMEM((width, panels), BF16),
             pltpu.VMEM((boxes, 8, panels), F32),
             pltpu.VMEM((boxes, FEAT, panels), BF16),
             pltpu.VMEM((boxes // 4, panels, 4 * FEAT), BF16),
@@ -406,6 +434,7 @@
             pltpu.VMEM((n_oct, slots + 16, width), BF16),
             pltpu.VMEM((klist, boxes, width), F32),
             pltpu.VMEM((boxes, n_pat * width), BF16),
+            dma((11,)),
             dma((6,)),
             dma((1,)),
             dma((chips,)),
@@ -418,21 +447,21 @@
             dma((n_oct,)),
         ],
         compiler_params=pltpu.CompilerParams(
-            collective_id=0, has_side_effects=True, vmem_limit_bytes=48 << 20
+            collective_id=0, has_side_effects=True, vmem_limit_bytes=62 << 20
         ),
     )(
-        near_boxes.T,
-        group_sources.T,
         positions,
         charges,
         panel_counts.reshape(boxes // 128, 128),
         moment_map,
         translations,
-        evaluation,
-        group_patterns.T,
         sources,
         patterns,
+        near_boxes.T,
         remote_targets[0, 0],
+        group_sources.T,
+        group_patterns.T,
+        evaluation,
     )
 
 

time: 50.2 us -> 37.9 us (0.75)
  the two profiles are of different devices: /device:TPU:8 before, /device:TPU:10 now
where the time goes in v2:
time: 37.9 us; the launch traced here: 37.8 us
  Pallas kernels  36.2 us (96%)
  local copies, waits for them, and re-layouts  1.57 us (4%)
    pallas_call x1, Pallas kernels, body(): pl.pallas_call(functools.partial(step_kernel, n_oct, n_cube), out_shape=j...  36.2 us
    unnamed x1, local copies, waits for them, and re-layouts  1.57 us

profile of v2, /device:TPU:10, one launch (start us, length us, event | category | flops | bytes accessed | tf_op | source)
XLA Modules:
  0.0 37.8 jit_solution(7901255297364644816)
XLA Ops:
  0.0 36.2 %shard_map.118 = f32[256,128]{1,0:T(8,128)} custom-call(f32[3,256,128]{2,1,0:T(8,128)} %pos_ref.1, bf16[256,128]{1,0:T(8,128)(2,1)} %charges_in.1, s32[2,128]{1,0:T(2,128)} %bitcast.17, bf16[128,128]{1,0:T(8,128)(2,1)} %moment_in.1, bf16[16,128,128]{2,1,0:T(8,128)(2,1)} %trans_in.1, s32[16,4,64]{2,1,0:T(4,128)} %bitcast.11, s32[16,4,64]{2,1,0:T(4,128)} %bitcast.12, ...), custom_call_target="tpu_custom_call" | custom-call | tf_op jit(solution)/shard_map/pallas_call | solution.py:403
  36.3 1.6 %copy.14 = f32[256,128]{1,0:T(8,128)} copy(f32[256,128]{1,0:T(8,128)} %shard_map.118) | data formatting | bytes 262144

commit v3 on v2

--- a/solution.py
+++ b/solution.py
@@ -13,7 +13,8 @@
 FEAT = 32
 SOFT = 0.0025
 NEAR_UNROLL = 32
-RING_FROM = 2
+CHIP_SENDS = ((0, 1), (0, -1), (0, 2), (0, -2), (-2, 1), (-2, 2), (2, -1))
+PASS_ON = (((6, 6), (2, 3, 0, 1)), ((7, 0), (4, 5, 6)))
 
 
 def parts3(v):
@@ -138,13 +139,12 @@
     got,
     rows_ref,
     sums_ref,
+    remote_ref,
     in_sem,
     pos_sem,
     key_sem,
-    right_send,
-    right_recv,
-    left_send,
-    left_recv,
+    chip_send,
+    chip_recv,
     sib_send,
     sib_recv,
     oct_send,
@@ -158,9 +158,6 @@
     klist = gs_ref.shape[0]
     fanin = rs_ref.shape[1]
     slots = rs_ref.shape[2]
-    chips = n_cube // 2
-    right = lax.rem(c + 2, n_cube)
-    left = lax.rem(c + n_cube - 2, n_cube)
     sib = c + 1 - 2 * lax.rem(c, 2)
 
     pairs = (
@@ -186,7 +183,8 @@
         copy.start()
 
     barrier = pltpu.get_barrier_semaphore()
-    for peer in (right, left, sib):
+    dests = sorted({d % (n_cube // 2) for _, d in CHIP_SENDS} | {-d % (n_cube // 2) for _, d in CHIP_SENDS})
+    for peer in [sib] + [lax.rem(c + 2 * d, n_cube) for d in dests]:
         pl.semaphore_signal(barrier, inc=1, device_id={"cube": peer}, device_id_type=MESH)
     for i in range(n_oct - 1):
         d = lax.rem(o + 1 + i, n_oct)
@@ -250,9 +248,11 @@
         for h in range(boxes // 128):
             pat_b[k, 128 * h : 128 * h + 128] = column(gp_ref[k : k + 1, 128 * h : 128 * h + 128])
 
-    pl.semaphore_wait(barrier, 3 + n_oct - 1)
-
-    def send(shard, peer, sends, recvs, n):
+    def shard_at(off):
+        return lax.rem(c + 2 * off + n_cube, n_cube)
+
+    def send(off, peer, sends, recvs, n):
+        shard = shard_at(off)
         return pltpu.make_async_remote_copy(
             src_ref=gall.at[shard],
             dst_ref=gall.at[shard],
@@ -262,34 +262,25 @@
             device_id_type=MESH,
         )
 
-    n_right = chips // 2
-    n_left = chips - 1 - n_right
-    from_left = [lax.rem(c + n_cube - 2 * h, n_cube) for h in range(n_right + 1)]
-    from_right = [lax.rem(c + 2 * h, n_cube) for h in range(n_left + 1)]
-    to_right = [send(from_left[h], right, right_send, right_recv, h) for h in range(n_right)]
-    to_left = [send(from_right[h], left, left_send, left_recv, h) for h in range(n_left)]
-    to_sib = [send(from_left[h], sib, sib_send, sib_recv, h) for h in range(n_right + 1)]
-    to_sib += [
-        send(from_right[h], sib, sib_send, sib_recv, n_right + h) for h in range(1, n_left + 1)
-    ]
-
-    to_right[0].start()
-    to_left[0].start()
-    to_sib[0].start()
-
-    def ring_step(h):
-        if h <= n_right:
-            to_right[h - 1].wait_recv()
-        if h <= n_left:
-            to_left[h - 1].wait_recv()
-        if h < n_right:
-            to_right[h].start()
-        if h < n_left:
-            to_left[h].start()
-        if h <= n_right:
-            to_sib[h].start()
-        if h <= n_left:
-            to_sib[n_right + h].start()
+    to_chip = [send(s, shard_at(d), chip_send, chip_recv, n) for n, (s, d) in enumerate(CHIP_SENDS)]
+    brought = [s - d for s, d in CHIP_SENDS]
+    to_sib = [send(s, sib, sib_send, sib_recv, n) for n, s in enumerate(brought + [0])]
+
+    def widen(off, other):
+        shard = shard_at(off)
+        if other:
+            shard = shard + 1 - 2 * lax.rem(c, 2)
+        rows = pl.ds(pl.multiple_of(shard * boxes, boxes), boxes)
+        gf_ref[rows, :] = gall[shard].astype(F32)
+
+    def pass_on(arrived):
+        for n in arrived:
+            to_chip[n].wait_recv()
+            for m, (s, d) in enumerate(CHIP_SENDS):
+                if s != 0 and s == brought[n]:
+                    to_chip[m].start()
+            to_sib[n].start()
+            widen(brought[n], False)
 
     def to_oct(i):
         d = lax.rem(o + 1 + i, n_oct)
@@ -302,25 +293,55 @@
             device_id_type=MESH,
         )
 
-    for i in range(n_oct - 1):
-        to_oct(i).start()
     got[o] = msg[o]
 
+    def open_up():
+        pl.semaphore_wait(barrier, 1 + len(dests) + n_oct - 1)
+        for n, (s, d) in enumerate(CHIP_SENDS):
+            if s == 0:
+                to_chip[n].start()
+        to_sib[-1].start()
+        for i in range(n_oct - 1):
+            to_oct(i).start()
+
+    open_up()
+
     def near_step(i, carry):
-        for h in range(1, n_right + 1):
-
-            @pl.when(i == h + RING_FROM)
-            def _(h=h):
-                ring_step(h)
+        for when, arrived in PASS_ON:
+
+            @pl.when(i == when[0] - (c // 2) * when[1] // (n_cube // 2))
+            def _(arrived=arrived):
+                pass_on(arrived)
 
         near_boxes_step(i, nb_ref, q_ref, src_b, tgt_b, near_ref, lane, sub)
         return carry
 
     lax.fori_loop(0, boxes // NEAR_UNROLL, near_step, 0)
 
-    for copy in to_sib:
-        copy.wait_recv()
-    gf_ref[...] = gall[...].reshape(n_cube * boxes, width).astype(F32)
+    for i in range(n_oct - 1):
+        to_oct(i).wait_recv()
+    box = lax.broadcasted_iota(I32, (boxes, 2 * slots), 0).astype(F32)
+    remote = None
+    for m in range(n_oct // 4):
+        hot, vals = [], []
+        for e in (4 * m, 4 * m + 2):
+            trow = got[e, slots : slots + 16, :].astype(F32) + got[
+                e + 1, slots : slots + 16, :
+            ].astype(F32)
+            hot.append(jnp.where(box == trow[0:1], 1.0, 0.0).astype(BF16))
+            vals += [got[e, 0:slots, :], got[e + 1, 0:slots, :]]
+        part = jnp.dot(
+            jnp.concatenate(hot, axis=1),
+            jnp.concatenate(vals, axis=0),
+            preferred_element_type=F32,
+        )
+        remote = part if remote is None else remote + part
+    remote_ref[...] = remote
+
+    widen(0, False)
+    for n, off in enumerate(brought + [0]):
+        to_sib[n].wait_recv()
+        widen(off, True)
 
     def gather(i, carry):
         t0 = pl.multiple_of(16 * i, 16)
@@ -345,31 +366,14 @@
 
     lax.fori_loop(0, boxes // 16, pattern_sums, 0)
     operators = trans_ref[...].reshape(n_pat * width, width)
-    local = jnp.dot(sums_ref[...], operators, preferred_element_type=F32)
-
-    for i in range(n_oct - 1):
-        to_oct(i).wait_recv()
-    box = lax.broadcasted_iota(I32, (boxes, 2 * slots), 0).astype(F32)
-    for m in range(n_oct // 4):
-        hot, vals = [], []
-        for e in (4 * m, 4 * m + 2):
-            trow = got[e, slots : slots + 16, :].astype(F32) + got[
-                e + 1, slots : slots + 16, :
-            ].astype(F32)
-            hot.append(jnp.where(box == trow[0:1], 1.0, 0.0).astype(BF16))
-            vals += [got[e, 0:slots, :], got[e + 1, 0:slots, :]]
-        local = local + jnp.dot(
-            jnp.concatenate(hot, axis=1),
-            jnp.concatenate(vals, axis=0),
-            preferred_element_type=F32,
-        )
+    local = jnp.dot(sums_ref[...], operators, preferred_element_type=F32) + remote_ref[...]
 
     far = jnp.dot(local.astype(BF16), eval_ref[...], preferred_element_type=F32)
     total = near_ref[...] * (1.0 / (4.0 * math.pi)) + far
     panel = lax.broadcasted_iota(I32, (boxes, panels), 1)
     out_ref[...] = jnp.where(panel < count_b[...], total, 0.0)
 
-    for copy in to_right + to_left + to_sib:
+    for copy in to_chip + to_sib:
         copy.wait_send()
     for i in range(n_oct - 1):
         to_oct(i).wait_send()
@@ -434,11 +438,10 @@
             pltpu.VMEM((n_oct, slots + 16, width), BF16),
             pltpu.VMEM((klist, boxes, width), F32),
             pltpu.VMEM((boxes, n_pat * width), BF16),
+            pltpu.VMEM((boxes, width), F32),
             dma((11,)),
             dma((6,)),
             dma((1,)),
-            dma((chips,)),
-            dma((chips,)),
             dma((chips,)),
             dma((chips,)),
             dma((chips,)),

time: 37.9 us -> 32 us (0.84)
  the two profiles are of different devices: /device:TPU:10 before, /device:TPU:1 now
where the time goes in v3:
time: 32 us; the launch traced here: 31.9 us
  Pallas kernels  30.3 us (95%)
  local copies, waits for them, and re-layouts  1.57 us (5%)
    pallas_call x1, Pallas kernels, body(): pl.pallas_call(functools.partial(step_kernel, n_oct, n_cube), out_shape=j...  30.3 us
    unnamed x1, local copies, waits for them, and re-layouts  1.57 us

profile of v3, /device:TPU:1, one launch (start us, length us, event | category | flops | bytes accessed | tf_op | source)
XLA Modules:
  0.0 31.9 jit_solution(9208777787038369488)
XLA Ops:
  0.0 30.3 %shard_map.118 = f32[256,128]{1,0:T(8,128)} custom-call(f32[3,256,128]{2,1,0:T(8,128)} %pos_ref.1, bf16[256,128]{1,0:T(8,128)(2,1)} %charges_in.1, s32[2,128]{1,0:T(2,128)} %bitcast.17, bf16[128,128]{1,0:T(8,128)(2,1)} %moment_in.1, bf16[16,128,128]{2,1,0:T(8,128)(2,1)} %trans_in.1, s32[16,4,64]{2,1,0:T(4,128)} %bitcast.11, s32[16,4,64]{2,1,0:T(4,128)} %bitcast.12, ...), custom_call_target="tpu_custom_call" | custom-call | tf_op jit(solution)/shard_map/pallas_call | solution.py:407
  30.3 1.6 %copy.14 = f32[256,128]{1,0:T(8,128)} copy(f32[256,128]{1,0:T(8,128)} %shard_map.118) | data formatting | bytes 262144

commit v4 on v3

--- a/solution.py
+++ b/solution.py
@@ -12,9 +12,9 @@
 MESH = pl.DeviceIdType.MESH
 FEAT = 32
 SOFT = 0.0025
-NEAR_UNROLL = 32
+BLOCK = 32
 CHIP_SENDS = ((0, 1), (0, -1), (0, 2), (0, -2), (-2, 1), (-2, 2), (2, -1))
-PASS_ON = (((6, 6), (2, 3, 0, 1)), ((7, 0), (4, 5, 6)))
+PASS_ON = (((5, 5), (2, 3, 0, 1)), ((7, 2), (4, 5, 6)))
 
 
 def parts3(v):
@@ -26,6 +26,10 @@
 
 def merge(a, b, first, shift, axis):
     return jnp.where(first, a, b) + pltpu.roll(jnp.where(first, b, a), shift, axis)
+
+
+def halves(word):
+    return word & 65535, lax.shift_right_logical(word, 16)
 
 
 def column(row):
@@ -59,15 +63,15 @@
 
 
 def near_boxes_step(i, nb_ref, q_ref, src_b, tgt_b, near_ref, lane, sub):
-    t0 = pl.multiple_of(NEAR_UNROLL * i, NEAR_UNROLL)
-    knear = nb_ref.shape[0]
+    t0 = pl.multiple_of(BLOCK * i, BLOCK)
     rows = []
-    for u in range(NEAR_UNROLL):
-        lhs = tgt_b[(NEAR_UNROLL // 4) * i + u // 4]
+    for u in range(BLOCK):
+        lhs = tgt_b[(BLOCK // 4) * i + u // 4]
         lo = FEAT * (u % 4)
         acc = None
-        for pair in range(knear // 2):
-            ids = [nb_ref[2 * pair + e, t0 + u] for e in range(2)]
+        word = nb_ref[i, 0, u]
+        for pair in range(2):
+            ids = [lax.shift_right_logical(word, 16 * pair + 8 * e) & 255 for e in range(2)]
             parts = [jnp.concatenate([src_b[s] for s in ids], axis=1)]
             if lo:
                 parts.insert(0, jnp.zeros((lo, 256), BF16))
@@ -85,7 +89,7 @@
             x = jnp.where(lane == sub + 8 * g, total, 0.0)
             row = x if row is None else row + x
         rows.append(row)
-    for b in range(NEAR_UNROLL // 8):
+    for b in range(BLOCK // 8):
         some = rows[8 * b : 8 * b + 8]
         shift = 1
         while len(some) > 1:
@@ -122,13 +126,16 @@
     gs_ref,
     gp_ref,
     eval_ref,
+    nb_v,
+    nb_s,
+    gs_v,
+    gs_s,
     p_ref,
     src_b,
     tgt_b,
     q_ref,
     near_ref,
     count_b,
-    pat_b,
     gall,
     gf_ref,
     table,
@@ -137,7 +144,9 @@
     slot_f,
     msg,
     got,
-    rows_ref,
+    rows_a,
+    rows_b,
+    hot_ref,
     sums_ref,
     remote_ref,
     in_sem,
@@ -195,7 +204,8 @@
 
     for copy in copies[:5]:
         copy.wait()
-    key_v[...] = rp_ref[...] * boxes + rs_ref[...]
+    key = rp_ref[...] * boxes + rs_ref[...]
+    key_v[...] = key[:, : fanin // 2] + key[:, fanin // 2 :] * 65536
     key_copy = pltpu.make_async_copy(key_v, key_s, key_sem.at[0])
     key_copy.start()
     lane_big = lax.broadcasted_iota(I32, (128, 128), 1)
@@ -209,6 +219,23 @@
     gall[c] = multipole
     for copy in copies[5:]:
         copy.wait()
+    index_copies = []
+    def four_bytes(v):
+        return v[0:1] + v[1:2] * 256 + v[2:3] * 65536 + v[3:4] * 16777216
+
+    def two_halves(v):
+        return v[: klist // 2] + v[klist // 2 :] * 65536
+
+    lists = ((nb_ref, nb_v, nb_s, four_bytes), (gs_ref, gs_v, gs_s, two_halves))
+    for n, (whole, cut, scalar, packed) in enumerate(lists):
+        for h in range(boxes // 128):
+            entries = whole[:, 128 * h : 128 * h + 128]
+            for e in range(128 // BLOCK):
+                turn = (128 - BLOCK * e) % 128
+                mine = pltpu.roll(entries, turn, 1) if turn else entries
+                cut[h * (128 // BLOCK) + e] = packed(mine)
+        index_copies.append(pltpu.make_async_copy(cut, scalar, key_sem.at[1 + n]))
+        index_copies[-1].start()
     for p in range(n_pat):
         table[p * boxes : (p + 1) * boxes] = jnp.dot(
             multipole, trans_ref[p], preferred_element_type=F32
@@ -229,14 +256,17 @@
             target_rows[d : d + 1], (16, 2 * slots)
         ).astype(BF16)
     key_copy.wait()
+    for copy in index_copies:
+        copy.wait()
     groups_each = boxes // (4 * n_oct)
 
     def one_group(d, carry):
         for j in range(slots):
             total = None
-            for k in range(fanin):
-                row = table[pl.ds(key_s[d, k, j], 1), :]
-                total = row if total is None else total + row
+            for k in range(fanin // 2):
+                for at in halves(key_s[d, k, j]):
+                    row = table[pl.ds(at, 1), :]
+                    total = row if total is None else total + row
             slot_f[j : j + 1, :] = total
         for u in range(groups_each):
             features_of_four(d * groups_each + u, p_ref, src_b, tgt_b, sub)
@@ -244,10 +274,6 @@
         return carry
 
     lax.fori_loop(0, n_oct, one_group, 0)
-    for k in range(klist):
-        for h in range(boxes // 128):
-            pat_b[k, 128 * h : 128 * h + 128] = column(gp_ref[k : k + 1, 128 * h : 128 * h + 128])
-
     def shard_at(off):
         return lax.rem(c + 2 * off + n_cube, n_cube)
 
@@ -306,6 +332,25 @@
 
     open_up()
 
+    lane_row = lax.broadcasted_iota(I32, (1, 128), 1)
+    lane_blk = lax.broadcasted_iota(I32, (BLOCK, 128), 1)
+    own = lax.rem(lane_blk, BLOCK) == lax.broadcasted_iota(I32, (BLOCK, 128), 0)
+    per = 128 // BLOCK
+    for h in range(boxes // 128):
+        entries = gp_ref[:, 128 * h : 128 * h + 128]
+        turned = [entries] + [pltpu.roll(entries, BLOCK * s, 1) for s in range(1, per)]
+        for e in range(per):
+            for half in range(klist // per):
+                row = None
+                for j in range(per):
+                    piece = turned[(j - e) % per][per * half + j : per * half + j + 1]
+                    row = piece if row is None else jnp.where(lane_row // BLOCK == j, piece, row)
+                wanted = jnp.where(own, row, -1)
+                for p in range(n_pat):
+                    hot_ref[per * h + e, BLOCK * p : BLOCK * (p + 1), 128 * half : 128 * half + 128] = (
+                        jnp.where(wanted == p, 1.0, 0.0).astype(BF16)
+                    )
+
     def near_step(i, carry):
         for when, arrived in PASS_ON:
 
@@ -313,10 +358,10 @@
             def _(arrived=arrived):
                 pass_on(arrived)
 
-        near_boxes_step(i, nb_ref, q_ref, src_b, tgt_b, near_ref, lane, sub)
+        near_boxes_step(i, nb_s, q_ref, src_b, tgt_b, near_ref, lane, sub)
         return carry
 
-    lax.fori_loop(0, boxes // NEAR_UNROLL, near_step, 0)
+    lax.fori_loop(0, boxes // BLOCK, near_step, 0)
 
     for i in range(n_oct - 1):
         to_oct(i).wait_recv()
@@ -343,28 +388,36 @@
         to_sib[n].wait_recv()
         widen(off, True)
 
-    def gather(i, carry):
-        t0 = pl.multiple_of(16 * i, 16)
-        for u in range(16):
-            for k in range(klist):
-                rows_ref[k, pl.ds(t0 + u, 1), :] = gf_ref[pl.ds(gs_ref[k, t0 + u], 1), :]
+    def gather(blk, rows_ref, ks):
+        for k in ks:
+            for u in range(BLOCK):
+                for e, at in enumerate(halves(gs_s[blk, k, u])):
+                    place = (k + e * klist // 2) * BLOCK + u
+                    rows_ref[place : place + 1, :] = gf_ref[pl.ds(at, 1), :]
+
+    def pattern_sums(blk, vals, ps):
+        t0 = pl.ds(pl.multiple_of(blk * BLOCK, BLOCK), BLOCK)
+        total = jnp.dot(hot_ref[blk, BLOCK * ps[0] : BLOCK * (ps[-1] + 1), :], vals, preferred_element_type=F32)
+        for n, p in enumerate(ps):
+            sums_ref[t0, p * width : (p + 1) * width] = total[BLOCK * n : BLOCK * (n + 1)].astype(
+                BF16
+            )
+
+    def both(nxt, nxt_ref, now, now_ref):
+        vals = now_ref[...].astype(BF16)
+        for k in range(klist // 2):
+            gather(nxt, nxt_ref, (k,))
+            pattern_sums(now, vals, tuple(range(2 * k * n_pat // klist, 2 * (k + 1) * n_pat // klist)))
+
+    blocks = boxes // BLOCK
+    gather(0, rows_a, range(klist // 2))
+
+    def two_blocks(i, carry):
+        both(2 * i + 1, rows_b, 2 * i, rows_a)
+        both(jnp.minimum(2 * i + 2, blocks - 1), rows_a, 2 * i + 1, rows_b)
         return carry
 
-    lax.fori_loop(0, boxes // 16, gather, 0)
-
-    def pattern_sums(i, carry):
-        t0 = pl.ds(pl.multiple_of(16 * i, 16), 16)
-        pats = [pat_b[k, t0] for k in range(klist)]
-        rows = [rows_ref[k, t0] for k in range(klist)]
-        for p in range(n_pat):
-            total = None
-            for k in range(klist):
-                x = jnp.where(pats[k] == p, rows[k], 0.0)
-                total = x if total is None else total + x
-            sums_ref[t0, p * width : (p + 1) * width] = total.astype(BF16)
-        return carry
-
-    lax.fori_loop(0, boxes // 16, pattern_sums, 0)
+    lax.fori_loop(0, blocks // 2, two_blocks, 0)
     operators = trans_ref[...].reshape(n_pat * width, width)
     local = jnp.dot(sums_ref[...], operators, preferred_element_type=F32) + remote_ref[...]
 
@@ -416,32 +469,37 @@
             pltpu.VMEM((n_pat, width, width), BF16),
             pltpu.VMEM((n_oct, fanin, slots), I32),
             pltpu.VMEM((n_oct, fanin, slots), I32),
-            pltpu.SMEM((near_boxes.shape[1], boxes), I32),
+            pltpu.VMEM((near_boxes.shape[1], boxes), I32),
             pltpu.VMEM((n_oct, slots), I32),
-            pltpu.SMEM((klist, boxes), I32),
+            pltpu.VMEM((klist, boxes), I32),
             pltpu.VMEM((klist, boxes), I32),
             pltpu.VMEM((width, panels), BF16),
+            pltpu.VMEM((boxes // BLOCK, 1, 128), I32),
+            pltpu.SMEM((boxes // BLOCK, 1, 128), I32),
+            pltpu.VMEM((boxes // BLOCK, klist // 2, 128), I32),
+            pltpu.SMEM((boxes // BLOCK, klist // 2, 128), I32),
             pltpu.VMEM((boxes, 8, panels), F32),
             pltpu.VMEM((boxes, FEAT, panels), BF16),
             pltpu.VMEM((boxes // 4, panels, 4 * FEAT), BF16),
             pltpu.VMEM((boxes, panels), F32),
             pltpu.VMEM((boxes, panels), F32),
             pltpu.VMEM((boxes, panels), I32),
-            pltpu.VMEM((klist, boxes, width), I32),
             pltpu.VMEM((n_cube, boxes, width), BF16),
             pltpu.VMEM((n_cube * boxes, width), F32),
             pltpu.VMEM((n_pat * boxes, width), F32),
-            pltpu.VMEM((n_oct, fanin, slots), I32),
-            pltpu.SMEM((n_oct, fanin, slots), I32),
+            pltpu.VMEM((n_oct, fanin // 2, slots), I32),
+            pltpu.SMEM((n_oct, fanin // 2, slots), I32),
             pltpu.VMEM((slots, width), F32),
             pltpu.VMEM((n_oct, slots + 16, width), BF16),
             pltpu.VMEM((n_oct, slots + 16, width), BF16),
-            pltpu.VMEM((klist, boxes, width), F32),
+            pltpu.VMEM((klist * BLOCK, width), F32),
+            pltpu.VMEM((klist * BLOCK, width), F32),
+            pltpu.VMEM((boxes // BLOCK, n_pat * BLOCK, klist * BLOCK), BF16),
             pltpu.VMEM((boxes, n_pat * width), BF16),
             pltpu.VMEM((boxes, width), F32),
             dma((11,)),
             dma((6,)),
-            dma((1,)),
+            dma((3,)),
             dma((chips,)),
             dma((chips,)),
             dma((chips,)),

time: 32 us -> 30.9 us (0.966)
  Pallas kernels: 30.3 us -> 29.2 us
    pallas_call x1, Pallas kernels: 30.3 us -> 29.2 us  [body(): pl.pallas_call(functools.partial(step_kernel, n_oct, n_cube), out_shape=j...]
where the time goes in v4:
time: 30.9 us; the launch traced here: 30.8 us
  Pallas kernels  29.2 us (94%)
  local copies, waits for them, and re-layouts  1.57 us (5%)
    pallas_call x1, Pallas kernels, body(): pl.pallas_call(functools.partial(step_kernel, n_oct, n_cube), out_shape=j...  29.2 us
    unnamed x1, local copies, waits for them, and re-layouts  1.57 us

profile of v4, /device:TPU:1, one launch (start us, length us, event | category | flops | bytes accessed | tf_op | source)
XLA Modules:
  0.0 30.8 jit_solution(9455542671912711386)
XLA Ops:
  0.0 29.2 %shard_map.118 = f32[256,128]{1,0:T(8,128)} custom-call(f32[3,256,128]{2,1,0:T(8,128)} %pos_ref.1, bf16[256,128]{1,0:T(8,128)(2,1)} %charges_in.1, s32[2,128]{1,0:T(2,128)} %bitcast.17, bf16[128,128]{1,0:T(8,128)(2,1)} %moment_in.1, bf16[16,128,128]{2,1,0:T(8,128)(2,1)} %trans_in.1, s32[16,4,64]{2,1,0:T(4,128)} %bitcast.11, s32[16,4,64]{2,1,0:T(4,128)} %bitcast.12, ...), custom_call_target="tpu_custom_call" | custom-call | tf_op jit(solution)/shard_map/pallas_call | solution.py:460
  29.2 1.6 %copy.14 = f32[256,128]{1,0:T(8,128)} copy(f32[256,128]{1,0:T(8,128)} %shard_map.118) | data formatting | bytes 262144

commit v5 on v4

--- a/solution.py
+++ b/solution.py
@@ -13,8 +13,8 @@
 FEAT = 32
 SOFT = 0.0025
 BLOCK = 32
-CHIP_SENDS = ((0, 1), (0, -1), (0, 2), (0, -2), (-2, 1), (-2, 2), (2, -1))
-PASS_ON = (((5, 5), (2, 3, 0, 1)), ((7, 2), (4, 5, 6)))
+CHIP_SENDS = ((0, 2), (0, -2), (0, 1), (0, -1), (-2, 1), (-2, 2), (2, -1))
+PASS_ON = (((5, 4), (0, 1, 2, 3), (7,)), ((7, 1), (4, 5, 6), (0, 1, 2, 3)))
 
 
 def parts3(v):
@@ -289,6 +289,9 @@
         )
 
     to_chip = [send(s, shard_at(d), chip_send, chip_recv, n) for n, (s, d) in enumerate(CHIP_SENDS)]
+    turn = 1 - 2 * lax.rem(c // 2, 2)
+    far = CHIP_SENDS.index((-2, 2))
+    to_chip[far] = send(-2 * turn, shard_at(2 * turn), chip_send, chip_recv, far)
     brought = [s - d for s, d in CHIP_SENDS]
     to_sib = [send(s, sib, sib_send, sib_recv, n) for n, s in enumerate(brought + [0])]
 
@@ -299,14 +302,20 @@
         rows = pl.ds(pl.multiple_of(shard * boxes, boxes), boxes)
         gf_ref[rows, :] = gall[shard].astype(F32)
 
-    def pass_on(arrived):
+    def pass_on(arrived, from_sib):
         for n in arrived:
             to_chip[n].wait_recv()
             for m, (s, d) in enumerate(CHIP_SENDS):
-                if s != 0 and s == brought[n]:
+                if s != 0 and s == brought[n] and m != far:
                     to_chip[m].start()
+            if brought[n] == 2:
+                to_chip[far].start()
             to_sib[n].start()
+        for n in arrived:
             widen(brought[n], False)
+        for n in from_sib:
+            to_sib[n].wait_recv()
+            widen((brought + [0])[n], True)
 
     def to_oct(i):
         d = lax.rem(o + 1 + i, n_oct)
@@ -352,11 +361,11 @@
                     )
 
     def near_step(i, carry):
-        for when, arrived in PASS_ON:
+        for when, arrived, from_sib in PASS_ON:
 
             @pl.when(i == when[0] - (c // 2) * when[1] // (n_cube // 2))
-            def _(arrived=arrived):
-                pass_on(arrived)
+            def _(arrived=arrived, from_sib=from_sib):
+                pass_on(arrived, from_sib)
 
         near_boxes_step(i, nb_s, q_ref, src_b, tgt_b, near_ref, lane, sub)
         return carry
@@ -385,8 +394,9 @@
 
     widen(0, False)
     for n, off in enumerate(brought + [0]):
-        to_sib[n].wait_recv()
-        widen(off, True)
+        if n not in PASS_ON[0][2] + PASS_ON[1][2]:
+            to_sib[n].wait_recv()
+            widen(off, True)
 
     def gather(blk, rows_ref, ks):
         for k in ks:
@@ -421,8 +431,8 @@
     operators = trans_ref[...].reshape(n_pat * width, width)
     local = jnp.dot(sums_ref[...], operators, preferred_element_type=F32) + remote_ref[...]
 
-    far = jnp.dot(local.astype(BF16), eval_ref[...], preferred_element_type=F32)
-    total = near_ref[...] * (1.0 / (4.0 * math.pi)) + far
+    far_field = jnp.dot(local.astype(BF16), eval_ref[...], preferred_element_type=F32)
+    total = near_ref[...] * (1.0 / (4.0 * math.pi)) + far_field
     panel = lax.broadcasted_iota(I32, (boxes, panels), 1)
     out_ref[...] = jnp.where(panel < count_b[...], total, 0.0)
 

time: 30.9 us -> 29.4 us (0.951)
  Pallas kernels: 29.2 us -> 27.7 us
    pallas_call x1, Pallas kernels: 29.2 us -> 27.7 us  [body(): pl.pallas_call(functools.partial(step_kernel, n_oct, n_cube), out_shape=j...]
where the time goes in v5:
time: 29.4 us; the launch traced here: 29.3 us
  Pallas kernels  27.7 us (94%)
  local copies, waits for them, and re-layouts  1.57 us (5%)
    pallas_call x1, Pallas kernels, body(): pl.pallas_call(functools.partial(step_kernel, n_oct, n_cube), out_shape=j...  27.7 us
    unnamed x1, local copies, waits for them, and re-layouts  1.57 us

profile of v5, /device:TPU:1, one launch (start us, length us, event | category | flops | bytes accessed | tf_op | source)
XLA Modules:
  0.0 29.3 jit_solution(17594645472212490026)
XLA Ops:
  0.0 27.7 %shard_map.118 = f32[256,128]{1,0:T(8,128)} custom-call(f32[3,256,128]{2,1,0:T(8,128)} %pos_ref.1, bf16[256,128]{1,0:T(8,128)(2,1)} %charges_in.1, s32[2,128]{1,0:T(2,128)} %bitcast.17, bf16[128,128]{1,0:T(8,128)(2,1)} %moment_in.1, bf16[16,128,128]{2,1,0:T(8,128)(2,1)} %trans_in.1, s32[16,4,64]{2,1,0:T(4,128)} %bitcast.11, s32[16,4,64]{2,1,0:T(4,128)} %bitcast.12, ...), custom_call_target="tpu_custom_call" | custom-call | tf_op jit(solution)/shard_map/pallas_call | solution.py:470
  27.7 1.6 %copy.14 = f32[256,128]{1,0:T(8,128)} copy(f32[256,128]{1,0:T(8,128)} %shard_map.118) | data formatting | bytes 262144

commit v6 on v5

--- a/solution.py
+++ b/solution.py
@@ -219,23 +219,6 @@
     gall[c] = multipole
     for copy in copies[5:]:
         copy.wait()
-    index_copies = []
-    def four_bytes(v):
-        return v[0:1] + v[1:2] * 256 + v[2:3] * 65536 + v[3:4] * 16777216
-
-    def two_halves(v):
-        return v[: klist // 2] + v[klist // 2 :] * 65536
-
-    lists = ((nb_ref, nb_v, nb_s, four_bytes), (gs_ref, gs_v, gs_s, two_halves))
-    for n, (whole, cut, scalar, packed) in enumerate(lists):
-        for h in range(boxes // 128):
-            entries = whole[:, 128 * h : 128 * h + 128]
-            for e in range(128 // BLOCK):
-                turn = (128 - BLOCK * e) % 128
-                mine = pltpu.roll(entries, turn, 1) if turn else entries
-                cut[h * (128 // BLOCK) + e] = packed(mine)
-        index_copies.append(pltpu.make_async_copy(cut, scalar, key_sem.at[1 + n]))
-        index_copies[-1].start()
     for p in range(n_pat):
         table[p * boxes : (p + 1) * boxes] = jnp.dot(
             multipole, trans_ref[p], preferred_element_type=F32
@@ -256,8 +239,6 @@
             target_rows[d : d + 1], (16, 2 * slots)
         ).astype(BF16)
     key_copy.wait()
-    for copy in index_copies:
-        copy.wait()
     groups_each = boxes // (4 * n_oct)
 
     def one_group(d, carry):
@@ -328,7 +309,6 @@
             device_id_type=MESH,
         )
 
-    got[o] = msg[o]
 
     def open_up():
         pl.semaphore_wait(barrier, 1 + len(dests) + n_oct - 1)
@@ -340,6 +320,25 @@
             to_oct(i).start()
 
     open_up()
+    got[o] = msg[o]
+
+    index_copies = []
+    def four_bytes(v):
+        return v[0:1] + v[1:2] * 256 + v[2:3] * 65536 + v[3:4] * 16777216
+
+    def two_halves(v):
+        return v[: klist // 2] + v[klist // 2 :] * 65536
+
+    lists = ((nb_ref, nb_v, nb_s, four_bytes), (gs_ref, gs_v, gs_s, two_halves))
+    for n, (whole, cut, scalar, packed) in enumerate(lists):
+        for h in range(boxes // 128):
+            entries = whole[:, 128 * h : 128 * h + 128]
+            for e in range(128 // BLOCK):
+                turn = (128 - BLOCK * e) % 128
+                mine = pltpu.roll(entries, turn, 1) if turn else entries
+                cut[h * (128 // BLOCK) + e] = packed(mine)
+        index_copies.append(pltpu.make_async_copy(cut, scalar, key_sem.at[1 + n]))
+        index_copies[-1].start()
 
     lane_row = lax.broadcasted_iota(I32, (1, 128), 1)
     lane_blk = lax.broadcasted_iota(I32, (BLOCK, 128), 1)
@@ -359,6 +358,9 @@
                     hot_ref[per * h + e, BLOCK * p : BLOCK * (p + 1), 128 * half : 128 * half + 128] = (
                         jnp.where(wanted == p, 1.0, 0.0).astype(BF16)
                     )
+
+    for copy in index_copies:
+        copy.wait()
 
     def near_step(i, carry):
         for when, arrived, from_sib in PASS_ON:

time: 29.4 us -> 28.8 us (0.980)
  Pallas kernels: 27.7 us -> 27.1 us
    pallas_call x1, Pallas kernels: 27.7 us -> 27.1 us  [body(): pl.pallas_call(functools.partial(step_kernel, n_oct, n_cube), out_shape=j...]
where the time goes in v6:
time: 28.8 us; the launch traced here: 28.7 us
  Pallas kernels  27.1 us (94%)
  local copies, waits for them, and re-layouts  1.57 us (5%)
    pallas_call x1, Pallas kernels, body(): pl.pallas_call(functools.partial(step_kernel, n_oct, n_cube), out_shape=j...  27.1 us
    unnamed x1, local copies, waits for them, and re-layouts  1.57 us

profile of v6, /device:TPU:1, one launch (start us, length us, event | category | flops | bytes accessed | tf_op | source)
XLA Modules:
  0.0 28.7 jit_solution(1973430541877790497)
XLA Ops:
  0.0 27.1 %shard_map.118 = f32[256,128]{1,0:T(8,128)} custom-call(f32[3,256,128]{2,1,0:T(8,128)} %pos_ref.1, bf16[256,128]{1,0:T(8,128)(2,1)} %charges_in.1, s32[2,128]{1,0:T(2,128)} %bitcast.17, bf16[128,128]{1,0:T(8,128)(2,1)} %moment_in.1, bf16[16,128,128]{2,1,0:T(8,128)(2,1)} %trans_in.1, s32[16,4,64]{2,1,0:T(4,128)} %bitcast.11, s32[16,4,64]{2,1,0:T(4,128)} %bitcast.12, ...), custom_call_target="tpu_custom_call" | custom-call | tf_op jit(solution)/shard_map/pallas_call | solution.py:472
  27.1 1.6 %copy.14 = f32[256,128]{1,0:T(8,128)} copy(f32[256,128]{1,0:T(8,128)} %shard_map.118) | data formatting | bytes 262144
